TPU v7x, 32 devices: a whole 2x2x4 slice. The times are simulated.
32 devices in a mesh: dp: 8 (over z, x), mp: 4 (over y, core).
Axes of the slice: x: 2, y: 2, z: 4, core: 2. Of those that a mesh axis runs over, the one named last changes fastest.
Arguments:
- tokens: bfloat16 [16384, 768], P('dp', 'mp'), may hold values from -6 to 6
- doc_ids: int32 [16, 1024], P('dp'), may hold values from 0 to 7, never falling along the last dimension, each value on 1 to 384 neighbouring positions
- positions_table: bfloat16 [1024, 768], replicated, may hold values from -3 to 3
- norm_gain: bfloat16 [2, 2, 768], replicated, may hold values from 0.5 to 1.5
- norm_shift: bfloat16 [2, 2, 768], replicated, may hold values from -1.5 to 1.5
- joined_projection_weight: bfloat16 [2, 768, 3, 768], P(None, None, None, 'mp'), may hold values from -0.21875 to 0.21875
- qv_bias: bfloat16 [2, 2, 768], P(None, None, 'mp'), may hold values from -1.5 to 1.5
- w_out: bfloat16 [2, 768, 768], P(None, 'mp'), may hold values from -0.625 to 0.625
- out_bias: bfloat16 [2, 2, 768], replicated, may hold values from -1.5 to 1.5
- w_fc: bfloat16 [2, 768, 3072], P(None, None, 'mp'), may hold values from -0.21875 to 0.21875
- fc_bias: bfloat16 [2, 3072], P(None, 'mp'), may hold values from -1.5 to 1.5
- w_proj: bfloat16 [2, 3072, 768], P(None, 'mp'), may hold values from -0.109375 to 0.109375
- cotangent: bfloat16 [16384, 768], P('dp', 'mp'), may hold values from -6 to 6
Outputs:
- out: bfloat16 [16384, 768], P('dp', 'mp')
- grad_tokens: float32 [16384, 768], P('dp', 'mp')
- grad_positions: float32 [1024, 768], P('dp', 'mp')
- grad_norm_gain: float32 [2, 2, 768], P(None, None, 'dp')
- grad_norm_shift: float32 [2, 2, 768], P(None, None, 'dp')
- joined_projection_gradient: float32 [2, 768, 3, 768], P(None, 'dp', None, 'mp')
- grad_qv_bias: float32 [2, 2, 768], P(None, None, ('mp', 'dp'))
- grad_w_out: float32 [2, 768, 768], P(None, 'mp', 'dp')
- grad_out_bias: float32 [2, 2, 768], P(None, None, 'dp')
- grad_w_fc: float32 [2, 768, 3072], P(None, 'dp', 'mp')
- grad_fc_bias: float32 [2, 3072], P(None, ('mp', 'dp'))
- grad_w_proj: float32 [2, 3072, 768], P(None, 'mp', 'dp')
Inputs may be any that keep to these rules, and one draw needn't show every extreme that they name: Along each packed row doc_ids never falls; every document has 1 to 384 tokens, and some document has exactly 384.
All inputs are finite; a program needn't handle non-finite values.
Results may differ from a plain program's by a relative error of at most 0.024.
Values may be sent and summed in bfloat16 or wider, within the bound.
No kernel may reach another device: no remote copies, remote signals or barrier semaphores. Data moves between devices by JAX's collectives and lax.ppermute only.
A program may use at most 256 MiB of HBM per device.

v0:
```python
import math

import jax
import jax.numpy as jnp
from jax import lax
from jax.sharding import PartitionSpec as P

HD = 64
LEN = 1024


epsilon = 1e-05


def layer_norm(stream, gain_row, shift_row):
    centred = stream - jnp.mean(stream, axis=-1, keepdims=True)
    variance = jnp.mean(centred * centred, axis=-1, keepdims=True)
    return centred * lax.rsqrt(variance + epsilon) * gain_row + shift_row


def doc_positions(doc_ids):
    row_index = jnp.broadcast_to(jnp.arange(doc_ids.shape[1], dtype=jnp.int32), doc_ids.shape)
    previous = jnp.concatenate([doc_ids[:, :1] - 1, doc_ids[:, :-1]], axis=1)
    starts = jnp.where(doc_ids != previous, row_index, 0)
    return row_index - lax.cummax(starts, axis=1)


def doc_mask(doc_row):
    row_index = jnp.arange(doc_row.shape[0], dtype=jnp.int32)
    return (doc_row[:, None] == doc_row[None, :]) & (row_index[None, :] <= row_index[:, None])


def masked_scores(queries, key_rows, doc_row):
    scale_factor = 1.0 / math.sqrt(HD)
    scores = (
        jnp.einsum("qhd,khd->hqk", queries, key_rows, preferred_element_type=jnp.float32)
        * scale_factor
    )
    return jnp.where(doc_mask(doc_row)[None], scores, -1e30)


def attend_block(pieces):
    queries, key_rows, value_rows, doc_row = pieces
    scores = masked_scores(queries, key_rows, doc_row)
    row_peak = jnp.max(scores, axis=-1, keepdims=True)
    exp_scores = jnp.exp(scores - row_peak)
    row_total = jnp.sum(exp_scores, axis=-1, keepdims=True)
    attn_probs = (exp_scores / row_total).astype(jnp.bfloat16)
    attended = jnp.einsum(
        "hqk,khd->qhd", attn_probs, value_rows, preferred_element_type=jnp.float32
    )
    return (attended.astype(jnp.bfloat16), (row_peak + jnp.log(row_total))[..., 0])


def attend_back(pieces):
    queries, key_rows, value_rows, doc_row, log_total, grad_attended = pieces
    scale_factor = 1.0 / math.sqrt(HD)
    scores = masked_scores(queries, key_rows, doc_row)
    attn_probs = jnp.exp(scores - log_total[..., None])
    grad_values = jnp.einsum(
        "hqk,qhd->khd",
        attn_probs.astype(jnp.bfloat16),
        grad_attended,
        preferred_element_type=jnp.float32,
    )
    grad_probs = jnp.einsum(
        "qhd,khd->hqk", grad_attended, value_rows, preferred_element_type=jnp.float32
    )
    inner_row_product = jnp.sum(attn_probs * grad_probs, axis=-1, keepdims=True)
    grad_scores = (attn_probs * (grad_probs - inner_row_product)).astype(jnp.bfloat16)
    grad_queries = (
        jnp.einsum("hqk,khd->qhd", grad_scores, key_rows, preferred_element_type=jnp.float32)
        * scale_factor
    )
    grad_keys = (
        jnp.einsum("hqk,qhd->khd", grad_scores, queries, preferred_element_type=jnp.float32)
        * scale_factor
    )
    return (
        grad_queries.astype(jnp.bfloat16),
        grad_keys.astype(jnp.bfloat16),
        grad_values.astype(jnp.bfloat16),
    )


def attention_local(stream, params, doc_ids):
    norm_gain_vectors, norm_shifts, joined_projection_weight, qv_bias = (
        params[0],
        params[1],
        params[2],
        params[3],
    )
    total_token_count, model_width = stream.shape
    col_share = joined_projection_weight.shape[-1]
    heads_local = col_share // HD
    normalized_input = layer_norm(stream, norm_gain_vectors[0], norm_shifts[0]).astype(jnp.bfloat16)
    mixed_qkv = jnp.dot(
        normalized_input,
        joined_projection_weight.reshape(model_width, 3 * col_share),
        preferred_element_type=jnp.float32,
    ).reshape(total_token_count, 3, col_share)
    queries = (mixed_qkv[:, 0] + qv_bias[0]).astype(jnp.bfloat16)
    key_rows = mixed_qkv[:, 1].astype(jnp.bfloat16)
    value_rows = (mixed_qkv[:, 2] + qv_bias[1]).astype(jnp.bfloat16)
    attended, log_total = lax.map(
        attend_block,
        (
            queries.reshape(-1, LEN, heads_local, HD),
            key_rows.reshape(-1, LEN, heads_local, HD),
            value_rows.reshape(-1, LEN, heads_local, HD),
            doc_ids,
        ),
    )
    return (
        normalized_input,
        queries,
        key_rows,
        value_rows,
        attended.reshape(total_token_count, col_share),
        log_total,
    )


def mlp_local(middle, params):
    norm_gain_vectors, norm_shifts, w_fc, fc_bias = (params[0], params[1], params[6], params[7])
    normed2 = layer_norm(middle, norm_gain_vectors[1], norm_shifts[1]).astype(jnp.bfloat16)
    hidden = jnp.dot(normed2, w_fc, preferred_element_type=jnp.float32) + fc_bias
    activated = jax.nn.gelu(hidden, approximate=True).astype(jnp.bfloat16)
    return (normed2, hidden, activated)


def block_forward(stream, params, doc_ids):
    w_out, out_bias, w_proj = (params[4], params[5], params[8])
    normalized_input, queries, key_rows, value_rows, attended, log_total = attention_local(
        stream, params, doc_ids
    )
    attn_sum = lax.psum(
        jnp.dot(attended, w_out, preferred_element_type=jnp.float32).astype(jnp.bfloat16), "mp"
    ).astype(jnp.float32)
    middle = stream + attn_sum + out_bias[0]
    normed2, hidden, activated = mlp_local(middle, params)
    mlp_sum = lax.psum(
        jnp.dot(activated, w_proj, preferred_element_type=jnp.float32).astype(jnp.bfloat16), "mp"
    ).astype(jnp.float32)
    result = middle + mlp_sum + out_bias[1]
    return (
        result,
        (
            stream,
            middle,
            normalized_input,
            queries,
            key_rows,
            value_rows,
            attended,
            log_total,
            normed2,
            hidden,
            activated,
        ),
    )


def norm_backward(stream, norm_gain_vectors, norm_shifts, which, grad_normed):

    def normalize(values, gain_row, shift_row):
        return layer_norm(values, gain_row, shift_row)

    _, norm_pull = jax.vjp(
        normalize,
        stream,
        norm_gain_vectors[which].astype(jnp.float32),
        norm_shifts[which].astype(jnp.float32),
    )
    return norm_pull(grad_normed)


def block_backward(grad_result, kept, params, doc_ids):
    (
        stream,
        middle,
        normalized_input,
        queries,
        key_rows,
        value_rows,
        attended,
        log_total,
        normed2,
        hidden,
        activated,
    ) = kept
    (
        norm_gain_vectors,
        norm_shifts,
        joined_projection_weight,
        qv_bias,
        w_out,
        out_bias,
        w_fc,
        fc_bias,
        w_proj,
    ) = params
    total_token_count, col_share = attended.shape
    heads_local = col_share // HD
    grad_low = grad_result.astype(jnp.bfloat16)
    grad_bias_mlp = jnp.sum(grad_result, axis=0)
    grad_w_proj = jnp.einsum("tf,td->fd", activated, grad_low, preferred_element_type=jnp.float32)
    grad_act = jnp.einsum("td,fd->tf", grad_low, w_proj, preferred_element_type=jnp.float32)

    def gelu_value(values):
        return jax.nn.gelu(values, approximate=True)

    _, gelu_pull = jax.vjp(gelu_value, hidden)
    grad_hidden = gelu_pull(grad_act)[0].astype(jnp.bfloat16)
    grad_fc_bias = jnp.sum(grad_hidden.astype(jnp.float32), axis=0)
    grad_w_fc = jnp.einsum("td,tf->df", normed2, grad_hidden, preferred_element_type=jnp.float32)
    grad_normed2 = lax.psum(
        jnp.einsum("tf,df->td", grad_hidden, w_fc, preferred_element_type=jnp.float32).astype(
            jnp.bfloat16
        ),
        "mp",
    ).astype(jnp.float32)
    grad_mid, grad_gain2, grad_shift2 = norm_backward(
        middle, norm_gain_vectors, norm_shifts, 1, grad_normed2
    )
    grad_middle = grad_result + grad_mid
    middle_low = grad_middle.astype(jnp.bfloat16)
    grad_bias_attn = jnp.sum(grad_middle, axis=0)
    grad_w_out = jnp.einsum("tc,td->cd", attended, middle_low, preferred_element_type=jnp.float32)
    grad_attended = jnp.einsum(
        "td,cd->tc", middle_low, w_out, preferred_element_type=jnp.float32
    ).astype(jnp.bfloat16)
    grad_queries, grad_keys, grad_values = lax.map(
        attend_back,
        (
            queries.reshape(-1, LEN, heads_local, HD),
            key_rows.reshape(-1, LEN, heads_local, HD),
            value_rows.reshape(-1, LEN, heads_local, HD),
            doc_ids,
            log_total,
            grad_attended.reshape(-1, LEN, heads_local, HD),
        ),
    )
    blended_gradient = jnp.stack(
        [
            grad_queries.reshape(total_token_count, col_share),
            grad_keys.reshape(total_token_count, col_share),
            grad_values.reshape(total_token_count, col_share),
        ],
        axis=1,
    )
    joined_projection_gradient = jnp.einsum(
        "lv,lbu->vbu", normalized_input, blended_gradient, preferred_element_type=jnp.float32
    )
    grad_qv_bias = jnp.stack(
        [
            jnp.sum(blended_gradient[:, 0].astype(jnp.float32), axis=0),
            jnp.sum(blended_gradient[:, 2].astype(jnp.float32), axis=0),
        ]
    )
    grad_normed = lax.psum(
        jnp.einsum(
            "ylu,zlu->yz",
            blended_gradient,
            joined_projection_weight,
            preferred_element_type=jnp.float32,
        ).astype(jnp.bfloat16),
        "mp",
    ).astype(jnp.float32)
    grad_in, grad_gain1, grad_shift1 = norm_backward(
        stream, norm_gain_vectors, norm_shifts, 0, grad_normed
    )
    grad_stream = grad_middle + grad_in
    grads = (
        jnp.stack([grad_gain1, grad_gain2]),
        jnp.stack([grad_shift1, grad_shift2]),
        joined_projection_gradient,
        grad_qv_bias,
        grad_w_out,
        jnp.stack([grad_bias_attn, grad_bias_mlp]),
        grad_w_fc,
        grad_fc_bias,
        grad_w_proj,
    )
    return (grad_stream, grads)


def on_device(
    tokens,
    doc_ids,
    positions_table,
    norm_gain,
    norm_shift,
    joined_projection_weight,
    qv_bias,
    w_out,
    out_bias,
    w_fc,
    fc_bias,
    w_proj,
    cotangent,
):
    full_tokens, full_cotangent = (
        lax.all_gather(tokens, "mp", axis=1, tiled=True),
        lax.all_gather(cotangent, "mp", axis=1, tiled=True),
    )
    places = doc_positions(doc_ids).reshape(-1)
    stream = full_tokens.astype(jnp.float32) + positions_table[places].astype(jnp.float32)
    student = (
        norm_gain[0],
        norm_shift[0],
        joined_projection_weight[0],
        qv_bias[0],
        w_out[0],
        out_bias[0],
        w_fc[0],
        fc_bias[0],
        w_proj[0],
    )
    teacher = (
        norm_gain[1],
        norm_shift[1],
        joined_projection_weight[1],
        qv_bias[1],
        w_out[1],
        out_bias[1],
        w_fc[1],
        fc_bias[1],
        w_proj[1],
    )
    middle_stream, kept_student = block_forward(stream, student, doc_ids)
    result, kept_teacher = block_forward(middle_stream, teacher, doc_ids)
    grad_mid, teacher_grads = block_backward(
        full_cotangent.astype(jnp.float32), kept_teacher, teacher, doc_ids
    )
    grad_stream, student_grads = block_backward(grad_mid, kept_student, student, doc_ids)
    col_share = tokens.shape[1]
    start = lax.axis_index("mp") * col_share
    grad_cols = lax.dynamic_slice_in_dim(grad_stream, start, col_share, 1)
    grad_table = jax.ops.segment_sum(grad_cols, places, num_segments=positions_table.shape[0])
    merged_result = tuple(
        (jnp.stack([first, second]) for first, second in zip(student_grads, teacher_grads))
    )
    all_sent = (
        lax.psum_scatter(
            merged_result[0].astype(jnp.bfloat16), "dp", scatter_dimension=2, tiled=True
        ).astype(jnp.float32),
        lax.psum_scatter(
            merged_result[1].astype(jnp.bfloat16), "dp", scatter_dimension=2, tiled=True
        ).astype(jnp.float32),
        lax.psum_scatter(
            merged_result[2].astype(jnp.bfloat16), "dp", scatter_dimension=1, tiled=True
        ).astype(jnp.float32),
        lax.psum_scatter(
            merged_result[3].astype(jnp.bfloat16), "dp", scatter_dimension=2, tiled=True
        ).astype(jnp.float32),
        lax.psum_scatter(
            merged_result[4].astype(jnp.bfloat16), "dp", scatter_dimension=2, tiled=True
        ).astype(jnp.float32),
        lax.psum_scatter(
            merged_result[5].astype(jnp.bfloat16), "dp", scatter_dimension=2, tiled=True
        ).astype(jnp.float32),
        lax.psum_scatter(
            merged_result[6].astype(jnp.bfloat16), "dp", scatter_dimension=1, tiled=True
        ).astype(jnp.float32),
        lax.psum_scatter(
            merged_result[7].astype(jnp.bfloat16), "dp", scatter_dimension=1, tiled=True
        ).astype(jnp.float32),
        lax.psum_scatter(
            merged_result[8].astype(jnp.bfloat16), "dp", scatter_dimension=2, tiled=True
        ).astype(jnp.float32),
        lax.psum_scatter(
            grad_table.astype(jnp.bfloat16), "dp", scatter_dimension=0, tiled=True
        ).astype(jnp.float32),
    )
    stacked = all_sent[:9]
    table_sent = all_sent[9]
    out_cols = lax.dynamic_slice_in_dim(result, start, col_share, 1).astype(jnp.bfloat16)
    return (
        out_cols,
        grad_cols,
        table_sent,
        stacked[0],
        stacked[1],
        stacked[2],
        stacked[3],
        stacked[4],
        stacked[5],
        stacked[6],
        stacked[7],
        stacked[8],
    )


def solution(mesh):
    in_specs = (
        P("dp", "mp"),
        P("dp", None),
        P(),
        P(),
        P(),
        P(None, None, None, "mp"),
        P(None, None, "mp"),
        P(None, "mp", None),
        P(),
        P(None, None, "mp"),
        P(None, "mp"),
        P(None, "mp", None),
        P("dp", "mp"),
    )
    out_specs = (
        P("dp", "mp"),
        P("dp", "mp"),
        P("dp", "mp"),
        P(None, None, "dp"),
        P(None, None, "dp"),
        P(None, "dp", None, "mp"),
        P(None, None, ("mp", "dp")),
        P(None, "mp", "dp"),
        P(None, None, "dp"),
        P(None, "dp", "mp"),
        P(None, ("mp", "dp")),
        P(None, "mp", "dp"),
    )
    return jax.shard_map(
        on_device, mesh=mesh, in_specs=in_specs, out_specs=out_specs, check_vma=False
    )
```

profile of v0, /device:TPU:0, one launch (start us, length us, event | category | flops | bytes accessed | tf_op | source)
XLA Modules:
  0.0 1649.4 jit_solution(230112099143261161)
XLA Ops:
  12.7 9.4 gather_fusion
  23.4 17.4 %all-gather.3.cloned.1.call-done = bf16[2048,768]{0,1:T(8,128)(2,1)} async-done(((bf16[2048,192]{0,1:T(8,128)(2,1)}), bf16[2048,768]{0,1:T(8,128)(2,1)}) %all-gather.3.cloned.1.call-update) | async-done | bytes 3145744 | tf_op jit(solution)/shard_map/all_gather | solution.py:304
  70.3 43.7 %while.52 = (s32[]{:T(128)}, bf16[2,1024,3,64]{1,3,2,0:T(8,128)(2,1)}, f32[2,3,1024]{2,1,0:T(4,128)S(1)}, bf16[2,1024,3,64]{1,3,2,0:T(8,128)(2,1)}, s32[2,1024]{...) while((s32[]{:T(128)}, ...), condition=%wide.region_7.8_spmd, body=%wide.region_4.7_spmd.sunk | while | flops 846394368 | bytes 53086392 | solution.py:105
  77.1 7.4 fusion.320
  84.6 6.8 fusion.321
  98.9 7.4 fusion.320
  106.3 6.8 fusion.321
  122.7 67.3 %all-reduce.12.cloned.1.call-done = bf16[2048,768]{1,0:T(8,128)(2,1)} async-done(((bf16[2048,768]{1,0:T(8,128)(2,1)}), bf16[2048,768]{1,0:T(8,128)(2,1)}) %all-reduce.12.cloned.1.call-update) | async-done | bytes 3145744 | tf_op jit(solution)/shard_map/psum | solution.py:137
  210.2 68.5 %all-reduce.14.cloned.1.call-done = bf16[2048,768]{1,0:T(8,128)(2,1)} async-done(((bf16[2048,768]{1,0:T(8,128)(2,1)}), bf16[2048,768]{1,0:T(8,128)(2,1)}) %all-reduce.14.cloned.1.call-update) | async-done | bytes 3145744 | tf_op jit(solution)/shard_map/psum | solution.py:142
  303.3 43.7 %while.53 = (s32[]{:T(128)}, bf16[2,1024,3,64]{1,3,2,0:T(8,128)(2,1)}, f32[2,3,1024]{2,1,0:T(4,128)S(1)}, bf16[2,1024,3,64]{1,3,2,0:T(8,128)(2,1)}, s32[2,1024]{...) while((s32[]{:T(128)}, ...), condition=%wide.region_17.18_spmd, body=%wide.region_14.17_spmd.sunk | while | flops 846394368 | bytes 53086392 | solution.py:105
  310.1 7.4 fusion.325
  317.5 6.8 fusion.326
  331.8 7.4 fusion.325
  339.3 6.8 fusion.326
  353.8 68.1 %all-reduce.16.cloned.1.call-done = bf16[2048,768]{1,0:T(8,128)(2,1)} async-done(((bf16[2048,768]{1,0:T(8,128)(2,1)}), bf16[2048,768]{1,0:T(8,128)(2,1)}) %all-reduce.16.cloned.1.call-update) | async-done | bytes 3145744 | tf_op jit(solution)/shard_map/psum | solution.py:137
  435.5 16.5 all-gather.5.cloned.1.call-done
  451.9 10.1 fusion.253
  472.4 63.9 %all-reduce.18.cloned.1.call-done = bf16[2048,768]{1,0:T(8,128)(2,1)} async-done(((bf16[2048,768]{1,0:T(8,128)(2,1)}), bf16[2048,768]{1,0:T(8,128)(2,1)}) %all-reduce.18.cloned.1.call-update) | async-done | bytes 3145744 | tf_op jit(solution)/shard_map/psum | solution.py:217
  559.0 49.9 %while.54 = (s32[]{:T(128)}, bf16[2,1024,3,64]{1,3,2,0:T(8,128)(2,1)}, bf16[2,1024,3,64]{1,3,2,0:T(8,128)(2,1)}, bf16[2,1024,3,64]{1,3,2,0:T(8,128)(2,1)}, bf16[...) while((s32[]{:T(128)}, ...), condition=%wide.region_27.28_spmd, body=%wide.region_25.27_spmd.sunk | while | flops 2064577536 | bytes 127776104 | solution.py:233
  565.5 7.2 multiply_reduce_fusion.8
  572.7 7.0 multiply_convert_fusion.10
  590.2 7.2 multiply_reduce_fusion.8
  597.5 7.0 multiply_convert_fusion.10
  622.5 68.7 %all-reduce.20.cloned.1.call-done = bf16[2048,768]{1,0:T(8,128)(2,1)} async-done(((bf16[2048,768]{1,0:T(8,128)(2,1)}), bf16[2048,768]{1,0:T(8,128)(2,1)}) %all-reduce.20.cloned.1.call-update) | async-done | bytes 3145744 | tf_op jit(solution)/shard_map/psum | solution.py:261
  707.6 8.1 fusion.254
  722.0 8.8 convolution_convert_fusion.2
  730.7 59.4 %all-reduce.22.cloned.1.call-done = bf16[2048,768]{1,0:T(8,128)(2,1)} async-done(((bf16[2048,768]{1,0:T(8,128)(2,1)}), bf16[2048,768]{1,0:T(8,128)(2,1)}) %all-reduce.22.cloned.1.call-update) | async-done | bytes 3145744 | tf_op jit(solution)/shard_map/psum | solution.py:217
  815.0 49.9 %while.55 = (s32[]{:T(128)}, bf16[2,1024,3,64]{1,3,2,0:T(8,128)(2,1)}, bf16[2,1024,3,64]{1,3,2,0:T(8,128)(2,1)}, bf16[2,1024,3,64]{1,3,2,0:T(8,128)(2,1)}, bf16[...) while((s32[]{:T(128)}, ...), condition=%wide.region_36.37_spmd, body=%wide.region_34.36_spmd.sunk | while | flops 2064577536 | bytes 127776104 | solution.py:233
  821.5 7.2 multiply_reduce_fusion.9
  828.7 7.0 multiply_convert_fusion.11
  846.3 7.2 multiply_reduce_fusion.9
  853.5 7.0 multiply_convert_fusion.11
  881.4 9.2 fusion.181
  891.6 9.3 fusion.182
  905.3 7.0 copy.119
  952.7 45.7 %all-reduce.26.cloned.1.call-done = (bf16[2048,768]{1,0:T(8,128)(2,1)}, bf16[2048,768]{1,0:T(8,128)(2,1)}) async-done(((bf16[2048,768]{1,0:T(8,128)(2,1)}, bf16[2048,768]{1,0:T(8,128)(2,1)}), (bf16[2048,768]{1,0:T(8,128)(2,1)}, bf16[2048,768]{1,0:T(8,128)(2,1)})) %all-reduce.26.cloned.1.call-update) | async-done | bytes 6291472 | tf_op jit(solution)/shard_map/psum | solution.py:261
  1015.3 7.0 reshape.720
  1025.9 38.4 %reduce-scatter.36.cloned.1.call-done = bf16[96,2]{1,0:T(8,128)(2,1)} async-done(((bf16[768,2]{1,0:T(8,128)(2,1)}), bf16[96,2]{1,0:T(8,128)(2,1)}) %reduce-scatter.36.cloned.1.call-update) | async-done | bytes 400
  1076.4 12.2 scatter_custom_fusion
  1089.5 19.4 %all-reduce = bf16[2,2,192]{2,1,0:T(2,128)(2,1)S(1)} all-reduce(bf16[2,2,192]{2,1,0:T(2,128)(2,1)S(1)} %pad_maximum_fusion.8), channel_id=6, replica_groups=mesh['dp'=8,'mp'=4] {'dp'}, use_global_device_ids=true, to_apply=%region_57.58.clone | all-reduce | flops 768 | bytes 3072
  1109.6 19.5 %reduce-scatter.34.cloned.1.call-done = bf16[96,4]{1,0:T(8,128)(2,1)} async-done(((bf16[768,4]{1,0:T(8,128)(2,1)}), bf16[96,4]{1,0:T(8,128)(2,1)}) %reduce-scatter.34.cloned.1.call-update) | async-done | bytes 784
  1130.7 109.6 %all-reduce.24.cloned.1.call-done = bf16[2,768,768]{1,0,2:T(2,128)(2,1)} async-done(((bf16[2,768,768]{1,0,2:T(2,128)(2,1)}), bf16[2,768,768]{1,0,2:T(2,128)(2,1)}) %all-reduce.24.cloned.1.call-update) | async-done | bytes 2359312
  1242.3 63.7 %reduce-scatter.32.cloned.1.call-done = bf16[96,384]{1,0:T(8,128)(2,1)} async-done(((bf16[768,384]{1,0:T(8,128)(2,1)}), bf16[96,384]{1,0:T(8,128)(2,1)}) %reduce-scatter.32.cloned.1.call-update) | async-done | bytes 73744
  1315.2 62.7 %reduce-scatter.24.cloned.1.call-done = bf16[2,96,768]{2,1,0:T(8,128)(2,1)} async-done(((bf16[2,768,768]{2,1,0:T(8,128)(2,1)}), bf16[2,96,768]{2,1,0:T(8,128)(2,1)}) %reduce-scatter.24.cloned.1.call-update) | async-done | bytes 294928 | tf_op jit(solution)/shard_map/reduce_scatter | solution.py:363
  1379.7 63.1 %reduce-scatter.26.cloned.1.call-done = bf16[96,4]{1,0:T(8,128)(2,1)} async-done(((bf16[768,4]{1,0:T(8,128)(2,1)}), bf16[96,4]{1,0:T(8,128)(2,1)}) %reduce-scatter.26.cloned.1.call-update) | async-done | bytes 784
  1444.3 62.6 %reduce-scatter.28.cloned.1.call-done = bf16[96,4]{1,0:T(8,128)(2,1)} async-done(((bf16[768,4]{1,0:T(8,128)(2,1)}), bf16[96,4]{1,0:T(8,128)(2,1)}) %reduce-scatter.28.cloned.1.call-update) | async-done | bytes 784
  1508.5 67.3 %reduce-scatter.30.cloned.1.call-done = bf16[96,1152]{1,0:T(8,128)(2,1)} async-done(((bf16[768,1152]{1,0:T(8,128)(2,1)}), bf16[96,1152]{1,0:T(8,128)(2,1)}) %reduce-scatter.30.cloned.1.call-update) | async-done | bytes 221200
  1578.4 62.2 %reduce-scatter.22.cloned.1.call-done = bf16[128,192]{1,0:T(8,128)(2,1)} async-done(((bf16[1024,192]{1,0:T(8,128)(2,1)}), bf16[128,192]{1,0:T(8,128)(2,1)}) %reduce-scatter.22.cloned.1.call-update) | async-done | bytes 49168 | tf_op jit(solution)/shard_map/reduce_scatter | solution.py:372
  (606 shorter events, 390.5 us)
Async XLA Ops:
  7.2 33.6 %all-gather.3.cloned.1.call-start = ((), (), s32[]{:S(2)}) async-start(), calls=%async_computation.8 | async-start | bytes 3932160 | tf_op jit(solution)/shard_map/all_gather | solution.py:304
  7.9 182.1 %all-reduce.12.cloned.1.call-start = ((), (), s32[]{:S(2)}) async-start(), calls=%async_computation.9 | async-start | bytes 6291456 | tf_op jit(solution)/shard_map/psum | solution.py:137
  22.8 29.7 %copy-start.84 = (f32[768]{0:T(1024)}, f32[768]{0:T(1024)S(1)}, u32[]{:S(2)}) copy-start(f32[768]{0:T(1024)S(1)} %get-tuple-element.354) | copy-start | bytes 9220
  117.4 77.8 %copy-start.18 = (bf16[24,8,2,1024]{3,1,2,0:T(8,128)(2,1)}, bf16[24,8,2,1024]{3,1,2,0:T(8,128)(2,1)S(1)}, u32[]{:S(2)}) copy-start(bf16[24,8,2,1024]{3,1,2,0:T(8,128)(2,1)S(1)} %copy.150) | copy-start | bytes 2359300
  121.4 157.2 %all-reduce.14.cloned.1.call-start = ((), (), s32[]{:S(2)}) async-start(), calls=%async_computation.10 | async-start | bytes 6291456 | tf_op jit(solution)/shard_map/psum | solution.py:142
  122.1 79.9 %copy-start.100 = (f32[768]{0:T(1024)}, f32[768]{0:T(1024)S(1)}, u32[]{:S(2)}) copy-start(f32[768]{0:T(1024)S(1)} %get-tuple-element.365) | copy-start | bytes 9220
  209.9 211.9 %all-reduce.16.cloned.1.call-start = ((), (), s32[]{:S(2)}) async-start(), calls=%async_computation.11 | async-start | bytes 6291456 | tf_op jit(solution)/shard_map/psum | solution.py:137
  349.0 72.9 %copy-start.92 = (f32[768]{0:T(1024)S(1)}, f32[768]{0:T(1024)}, u32[]{:S(2)}) copy-start(f32[768]{0:T(1024)} %get-tuple-element.363) | copy-start | bytes 9220
  349.2 77.3 %copy-start.20 = (bf16[24,8,2,1024]{3,1,2,0:T(8,128)(2,1)}, bf16[24,8,2,1024]{3,1,2,0:T(8,128)(2,1)S(1)}, u32[]{:S(2)}) copy-start(bf16[24,8,2,1024]{3,1,2,0:T(8,128)(2,1)S(1)} %copy.151) | copy-start | bytes 2359300
  353.2 98.8 %all-gather.5.cloned.1.call-start = ((), (), s32[]{:S(2)}) async-start(), calls=%async_computation.12 | async-start | bytes 3932160 | tf_op jit(solution)/shard_map/all_gather | solution.py:305
  353.8 182.5 %all-reduce.18.cloned.1.call-start = ((), (), s32[]{:S(2)}) async-start(), calls=%async_computation.13 | async-start | bytes 6291456 | tf_op jit(solution)/shard_map/psum | solution.py:217
  431.0 20.9 %copy-start.103 = (f32[768]{0:T(1024)S(1)}, f32[768]{0:T(1024)}, u32[]{:S(2)}) copy-start(f32[768]{0:T(1024)} %get-tuple-element.364) | copy-start | bytes 9220
  451.9 11.8 copy-start.112
  467.7 223.4 %all-reduce.20.cloned.1.call-start = ((), (), s32[]{:S(2)}) async-start(), calls=%async_computation.14 | async-start | bytes 6291456 | tf_op jit(solution)/shard_map/psum | solution.py:261
  617.2 74.0 %copy-start.62 = (f32[2048]{0:T(1024)S(1)}, f32[2048]{0:T(1024)}, u32[]{:S(2)}) copy-start(f32[2048]{0:T(1024)} %copy-done.61) | copy-start | bytes 24580
  617.2 74.0 %copy-start.76 = (f32[768]{0:T(1024)S(1)}, f32[768]{0:T(1024)}, u32[]{:S(2)}) copy-start(f32[768]{0:T(1024)} %get-tuple-element.355) | copy-start | bytes 9220
  622.4 73.4 %copy-start.83 = (f32[2048]{0:T(1024)S(1)}, f32[2048]{0:T(1024)}, u32[]{:S(2)}) copy-start(f32[2048]{0:T(1024)} %copy-done.82) | copy-start | bytes 24580
  622.4 73.4 %copy-start.70 = (f32[2048]{0:T(1024)S(1)}, f32[2048]{0:T(1024)}, u32[]{:S(2)}) copy-start(f32[2048]{0:T(1024)} %copy-done.69) | copy-start | bytes 24580
  622.4 167.7 %all-reduce.22.cloned.1.call-start = ((), (), s32[]{:S(2)}) async-start(), calls=%async_computation.15 | async-start | bytes 6291456 | tf_op jit(solution)/shard_map/psum | solution.py:217
  691.2 10.7 slice-start.2
  695.9 11.7 slice-start.6
  721.5 276.9 %all-reduce.26.cloned.1.call-start = ((), (), s32[]{:S(2)}) async-start(), calls=%async_computation.25 | async-start | bytes 12582912 | tf_op jit(solution)/shard_map/psum | solution.py:261
  721.9 68.2 %copy-start.60 = (f32[2048]{0:T(1024)S(1)}, f32[2048]{0:T(1024)}, u32[]{:S(2)}) copy-start(f32[2048]{0:T(1024)} %copy-done.59) | copy-start | bytes 24580
  721.9 68.2 %copy-start.74 = (f32[768]{0:T(1024)S(1)}, f32[768]{0:T(1024)}, u32[]{:S(2)}) copy-start(f32[768]{0:T(1024)} %get-tuple-element.353) | copy-start | bytes 9220
  730.7 64.1 %copy-start.81 = (f32[2048]{0:T(1024)S(1)}, f32[2048]{0:T(1024)}, u32[]{:S(2)}) copy-start(f32[2048]{0:T(1024)} %copy-done.80) | copy-start | bytes 24580
  730.7 64.1 %copy-start.68 = (f32[2048]{0:T(1024)S(1)}, f32[2048]{0:T(1024)}, u32[]{:S(2)}) copy-start(f32[2048]{0:T(1024)} %copy-done.67) | copy-start | bytes 24580
  790.2 10.7 slice-start
  878.5 185.8 %reduce-scatter.36.cloned.1.call-start = ((), (), s32[]{:S(2)}) async-start(), calls=%async_computation.23 | async-start | bytes 221184
  900.9 228.3 %reduce-scatter.34.cloned.1.call-start = ((), (), s32[]{:S(2)}) async-start(), calls=%async_computation.22 | async-start | bytes 221184
  901.4 11.0 copy-start.21
  902.3 337.9 %all-reduce.24.cloned.1.call-start = ((), (), s32[]{:S(2)}) async-start(), calls=%async_computation.24 | async-start | bytes 4718592
  905.3 10.8 copy-start.19
  912.4 393.6 %reduce-scatter.32.cloned.1.call-start = ((), (), s32[]{:S(2)}) async-start(), calls=%async_computation.21 | async-start | bytes 663552
  921.7 456.2 %reduce-scatter.24.cloned.1.call-start = ((), (), s32[]{:S(2)}) async-start(), calls=%async_computation.17 | async-start | bytes 2654208 | tf_op jit(solution)/shard_map/reduce_scatter | solution.py:363
  933.8 509.0 %reduce-scatter.26.cloned.1.call-start = ((), (), s32[]{:S(2)}) async-start(), calls=%async_computation.18 | async-start | bytes 221184
  946.6 54.2 %copy-start.66 = (f32[2048]{0:T(1024)S(1)}, f32[2048]{0:T(1024)}, u32[]{:S(2)}) copy-start(f32[2048]{0:T(1024)} %copy-done.65) | copy-start | bytes 24580
  946.6 54.1 %copy-start.72 = (f32[2048]{0:T(1024)S(1)}, f32[2048]{0:T(1024)}, u32[]{:S(2)}) copy-start(f32[2048]{0:T(1024)} %copy-done.71) | copy-start | bytes 24580
  946.6 54.1 %copy-start.85 = (f32[768]{0:T(1024)S(1)}, f32[768]{0:T(1024)}, u32[]{:S(2)}) copy-start(f32[768]{0:T(1024)} %copy-done.84) | copy-start | bytes 9220
  1008.2 498.8 %reduce-scatter.28.cloned.1.call-start = ((), (), s32[]{:S(2)}) async-start(), calls=%async_computation.19 | async-start | bytes 221184
  1009.6 566.2 %reduce-scatter.30.cloned.1.call-start = ((), (), s32[]{:S(2)}) async-start(), calls=%async_computation.20 | async-start | bytes 1990656
  1011.0 11.7 copy-start.118
  1011.0 14.3 copy-start.30
  1011.0 14.6 copy-start.34
  1011.0 55.2 %copy-start.79 = (f32[2048]{0:T(1024)S(1)}, f32[2048]{0:T(1024)}, u32[]{:S(2)}) copy-start(f32[2048]{0:T(1024)} %copy-done.78) | copy-start | bytes 24580
  1015.3 50.4 %copy-start.37 = (bf16[2,1024,3,64]{1,3,2,0:T(8,128)(2,1)S(1)}, bf16[2,1024,3,64]{1,3,2,0:T(8,128)(2,1)}, u32[]{:S(2)}) copy-start(bf16[2,1024,3,64]{1,3,2,0:T(8,128)(2,1)} %get-tuple-element.205) | copy-start | bytes 2359300
  1015.3 50.6 %copy-start.41 = (bf16[2,1024,3,64]{1,3,2,0:T(8,128)(2,1)S(1)}, bf16[2,1024,3,64]{1,3,2,0:T(8,128)(2,1)}, u32[]{:S(2)}) copy-start(bf16[2,1024,3,64]{1,3,2,0:T(8,128)(2,1)} %get-tuple-element.203) | copy-start | bytes 2359300
  1022.4 618.2 %reduce-scatter.22.cloned.1.call-start = ((), (), s32[]{:S(2)}) async-start(), calls=%async_computation.16 | async-start | bytes 589824 | tf_op jit(solution)/shard_map/reduce_scatter | solution.py:372
  1307.1 335.1 %copy-start.1 = (bf16[1024,768]{1,0:T(8,128)(2,1)S(1)}, bf16[1024,768]{1,0:T(8,128)(2,1)}, u32[]{:S(2)}) copy-start(bf16[1024,768]{1,0:T(8,128)(2,1)} %param.23) | copy-start | bytes 4718596
  (123 other events, 545.8 us)
Sparse Core Ops, SparseCore 0:
  9.6 31.2 all-gather.2
  121.5 68.4 all-reduce.11
  210.1 68.5 all-reduce.13
  353.3 68.5 all-reduce.15
  423.3 28.5 all-gather.4
  467.8 68.4 all-reduce.17
  622.6 68.5 all-reduce.19
  721.6 68.5 all-reduce.21
  878.6 119.7 all-reduce.25
  1002.0 62.2 reduce-scatter.35
  1068.1 61.0 reduce-scatter.33
  1132.6 107.6 all-reduce.23
  1244.1 61.8 reduce-scatter.31
  1309.3 68.5 reduce-scatter.23
  1381.6 61.1 reduce-scatter.25
  1445.9 61.0 reduce-scatter.27
  1510.3 65.4 reduce-scatter.29
  1579.0 61.5 reduce-scatter.21
where the time goes:
time: 1660 us; the launch traced here: 1650 us
  waiting for transfers between devices  1030 us (62%)
  matrix products  234 us (14%)
  other arithmetic  212 us (13%)
  local copies, waits for them, and re-layouts  136 us (8%)
  blocking collectives  19.4 us (1%)
  between operations  17.8 us (1%)
    unnamed x25, waiting for transfers between devices  426 us
    psum x2, waiting for transfers between devices, block_forward(): lax.psum(jnp.dot(attended, w_out, preferred_element_type=jnp.float32).ast...  135 us
    psum x2, waiting for transfers between devices, block_backward(): lax.psum(jnp.einsum('tf,df->td', grad_hidden, w_fc, preferred_element_typ...  123 us
    psum x2, waiting for transfers between devices, block_backward(): lax.psum(jnp.einsum('ylu,zlu->yz', blended_gradient, joined_projection_we...  114 us
    psum x1, waiting for transfers between devices, block_forward(): lax.psum(jnp.dot(activated, w_proj, preferred_element_type=jnp.float32).a...  68.5 us
    reduce_scatter x1, waiting for transfers between devices, on_device(): lax.psum_scatter(merged_result[6].astype(jnp.bfloat16), 'dp', scatter_dim...  62.7 us
    reduce_scatter x1, waiting for transfers between devices, on_device(): lax.psum_scatter(grad_table.astype(jnp.bfloat16), 'dp', scatter_dimension...  62.2 us
    unnamed x255, local copies, waits for them, and re-layouts  52.9 us
  transfers between devices with their start and end apart: 18, of which 18 were waited for; matrix products, arithmetic and copies ran while one was open for 11% of the time, Pallas kernels for 0%

commit v1 on v0

v1 whole, which is shorter than its diff:
```python
import functools
import math

import jax
import jax.numpy as jnp
from jax import lax
from jax.experimental import pallas as pl
from jax.experimental.pallas import tpu as pltpu
from jax.sharding import PartitionSpec as P

HD = 64
LEN = 1024
DOC_MOST = 384
EPS = 1e-05
BT = 256
QB = 128
KW = QB + DOC_MOST
F32 = jnp.float32
BF16 = jnp.bfloat16
GELU_C = math.sqrt(2.0 / math.pi)


def full_spec(shape):
    return pl.BlockSpec(shape, lambda g: (0,) * len(shape))


def rows_spec(width):
    return pl.BlockSpec((BT, width), lambda g: (g, 0))


def dot(a, b, ca=1, cb=0):
    return lax.dot_general(a, b, (((ca,), (cb,)), ((), ())), preferred_element_type=F32)


def normed_parts(v):
    centred = v - jnp.mean(v, axis=-1, keepdims=True)
    variance = jnp.mean(centred * centred, axis=-1, keepdims=True)
    rstd = lax.rsqrt(variance + EPS)
    return centred * rstd, rstd


def norm_back(g, own, oth, v, gain):
    grad = own.astype(F32) + oth.astype(F32)
    xhat, rstd = normed_parts(v)
    gn = grad * gain
    out = g + rstd * (
        gn
        - jnp.mean(gn, axis=-1, keepdims=True)
        - xhat * jnp.mean(gn * xhat, axis=-1, keepdims=True)
    )
    return out, grad * xhat, grad


def colsum(v):
    return jnp.sum(v, axis=0, keepdims=True)


def head_pair(block):
    lane = lax.broadcasted_iota(jnp.int32, block.shape, 1)
    zero = jnp.zeros_like(block)
    return jnp.concatenate(
        [jnp.where(lane < HD, block, zero), jnp.where(lane < HD, zero, block)], axis=0
    )


def window_bias(start_ref, i, ks):
    kidx = lax.broadcasted_iota(jnp.int32, (KW, QB), 0) + ks
    qidx = lax.broadcasted_iota(jnp.int32, (KW, QB), 1) + i * QB
    first = start_ref[0:1, pl.ds(pl.multiple_of(i * QB, QB), QB)]
    bias = jnp.where((kidx >= first) & (kidx <= qidx), 0.0, -1e30).astype(F32)
    return jnp.concatenate([bias, bias], axis=1)


def attn_fwd_kernel(layer, first, half, *refs):
    if first:
        (tok, emb, start, gain, shift, wqkv, qvb, wout) = refs[:8]
        rest = refs[8:]
        x = tok[...].astype(F32) + emb[...].astype(F32)
    else:
        (mid, own, oth, outb, start, gain, shift, wqkv, qvb, wout) = refs[:10]
        rest = refs[10:]
        x = (
            mid[...]
            + (own[...].astype(F32) + oth[...].astype(F32))
            + outb[layer - 1, 1:2, :].astype(F32)
        )
    x_o, n_o, qkv_o, att_o, lse_o, part_o, v_t, o_t = rest
    g = pl.program_id(0)

    @pl.when(g == 0)
    def _():
        qkv_o[pl.ds(BT, KW - BT), half : 2 * half] = jnp.zeros((KW - BT, half), BF16)
        v_t[:, pl.ds(BT, KW - BT)] = jnp.zeros((half, KW - BT), BF16)
        lse_o[...] = jnp.zeros_like(lse_o)

    x_o[...] = x
    xhat, _ = normed_parts(x)
    normed = (
        xhat * gain[layer, 0:1, :].astype(F32) + shift[layer, 0:1, :].astype(F32)
    ).astype(BF16)
    n_o[...] = normed
    qkv = dot(normed, wqkv[...])
    q = (qkv[:, :half] + qvb[layer, 0:1, :].astype(F32)).astype(BF16)
    k = qkv[:, half : 2 * half].astype(BF16)
    v = qkv[:, 2 * half :] + qvb[layer, 1:2, :].astype(F32)
    rows = pl.ds(pl.multiple_of(g * BT, BT), BT)
    qkv_o[rows, :half] = q
    qkv_o[rows, half : 2 * half] = k
    qkv_o[rows, 2 * half :] = v.astype(BF16)
    v_t[:, rows] = jnp.transpose(v).astype(BF16)
    q = q * jnp.asarray(1.0 / math.sqrt(HD), BF16)
    for s in range(BT // QB):
        i = g * (BT // QB) + s
        ks = pl.multiple_of(jnp.maximum(i - DOC_MOST // QB, 0) * QB, QB)
        bias = window_bias(start, i, ks)
        cols = pl.ds(pl.multiple_of(i * QB, QB), QB)
        for p in range(half // 128):
            lo = 128 * p
            qq = head_pair(q[QB * s : QB * (s + 1), lo : lo + 128])
            kp = qkv_o[pl.ds(ks, KW), half + lo : half + lo + 128]
            scores = dot(kp, qq, 1, 1) + bias
            peak = jnp.max(scores, axis=0, keepdims=True)
            e = jnp.exp(scores - peak)
            total = jnp.sum(e, axis=0, keepdims=True)
            ot = dot(v_t[lo : lo + 128, pl.ds(ks, KW)], e.astype(BF16))
            inv = 1.0 / total
            o_t[lo : lo + HD, :] = ot[:HD, :QB] * inv[:, :QB]
            o_t[lo + HD : lo + 128, :] = ot[HD:, QB:] * inv[:, QB:]
            lse = peak + jnp.log(total)
            lse_o[2 * p : 2 * p + 1, cols] = lse[:, :QB]
            lse_o[2 * p + 1 : 2 * p + 2, cols] = lse[:, QB:]
        att_o[QB * s : QB * (s + 1), :] = jnp.transpose(o_t[...]).astype(BF16)
    part_o[...] = dot(att_o[...], wout[...]).astype(BF16)


def attn_fwd(layer, stream_in, start, gain, shift, wqkv, qvb, wout, outb):
    first = layer == 0
    d = gain.shape[-1]
    half = wqkv.shape[1] // 3
    ins = list(stream_in)
    specs = [rows_spec(d) for _ in ins]
    if not first:
        ins.append(outb)
        specs.append(full_spec(outb.shape))
    for a in (start, gain, shift, wqkv, qvb, wout):
        ins.append(a)
        specs.append(full_spec(a.shape))
    return pl.pallas_call(
        functools.partial(attn_fwd_kernel, layer, first, half),
        grid=(LEN // BT,),
        in_specs=specs,
        out_specs=[
            rows_spec(d),
            rows_spec(d),
            full_spec((LEN, 3 * half)),
            rows_spec(half),
            full_spec((8, LEN)),
            rows_spec(d),
        ],
        out_shape=[
            jax.ShapeDtypeStruct((LEN, d), F32),
            jax.ShapeDtypeStruct((LEN, d), BF16),
            jax.ShapeDtypeStruct((LEN, 3 * half), BF16),
            jax.ShapeDtypeStruct((LEN, half), BF16),
            jax.ShapeDtypeStruct((8, LEN), F32),
            jax.ShapeDtypeStruct((LEN, d), BF16),
        ],
        scratch_shapes=[pltpu.VMEM((half, LEN), BF16), pltpu.VMEM((half, QB), F32)],
        name=f"attn_fwd_{layer}",
    )(*ins)


def mlp_fwd_kernel(layer, x, own, oth, outb, gain, shift, wfc, fcb, wproj, mid_o, n_o, h_o, part_o):
    mid = (
        x[...]
        + (own[...].astype(F32) + oth[...].astype(F32))
        + outb[layer, 0:1, :].astype(F32)
    )
    mid_o[...] = mid
    xhat, _ = normed_parts(mid)
    normed = (
        xhat * gain[layer, 1:2, :].astype(F32) + shift[layer, 1:2, :].astype(F32)
    ).astype(BF16)
    n_o[...] = normed
    hidden = dot(normed, wfc[...]) + fcb[layer : layer + 1, :].astype(F32)
    h_o[...] = hidden.astype(BF16)
    t = jnp.tanh(GELU_C * (hidden + 0.044715 * hidden * hidden * hidden))
    act = (0.5 * hidden * (1.0 + t)).astype(BF16)
    part_o[...] = dot(act, wproj[...]).astype(BF16)


def mlp_fwd(layer, x, own, oth, outb, gain, shift, wfc, fcb, wproj):
    d = x.shape[1]
    f = wfc.shape[1]
    ins = [x, own, oth, outb, gain, shift, wfc, fcb, wproj]
    specs = [rows_spec(d)] * 3 + [full_spec(a.shape) for a in ins[3:]]
    return pl.pallas_call(
        functools.partial(mlp_fwd_kernel, layer),
        grid=(LEN // BT,),
        in_specs=specs,
        out_specs=[rows_spec(d), rows_spec(d), rows_spec(f), rows_spec(d)],
        out_shape=[
            jax.ShapeDtypeStruct((LEN, d), F32),
            jax.ShapeDtypeStruct((LEN, d), BF16),
            jax.ShapeDtypeStruct((LEN, f), BF16),
            jax.ShapeDtypeStruct((LEN, d), BF16),
        ],
        name=f"mlp_fwd_{layer}",
    )(*ins)


def mlp_bwd_kernel(g, h, wfc, wproj, low_o, act_o, gh_o, part_o, sumg_o, sumh_o):
    step = pl.program_id(0)

    @pl.when(step == 0)
    def _():
        sumg_o[...] = jnp.zeros_like(sumg_o)
        sumh_o[...] = jnp.zeros_like(sumh_o)

    grad = g[...].astype(F32)
    low = grad.astype(BF16)
    low_o[...] = low
    grad_act = dot(low, wproj[...], 1, 1)
    v = h[...].astype(F32)
    v2 = v * v
    t = jnp.tanh(GELU_C * v * (1.0 + 0.044715 * v2))
    cdf = 0.5 * (1.0 + t)
    act_o[...] = (v * cdf).astype(BF16)
    slope = cdf + (0.5 * GELU_C) * v * (1.0 - t * t) * (1.0 + (3 * 0.044715) * v2)
    gh = (grad_act * slope).astype(BF16)
    gh_o[...] = gh
    part_o[...] = dot(gh, wfc[...], 1, 1).astype(BF16)
    sumg_o[0:1, :] += colsum(grad)
    sumh_o[0:1, :] += colsum(gh.astype(F32))


def mlp_bwd(layer, g, h, wfc, wproj):
    d, f = wfc.shape
    return pl.pallas_call(
        mlp_bwd_kernel,
        grid=(LEN // BT,),
        in_specs=[rows_spec(d), rows_spec(f), full_spec(wfc.shape), full_spec(wproj.shape)],
        out_specs=[
            rows_spec(d),
            rows_spec(f),
            rows_spec(f),
            rows_spec(d),
            full_spec((8, d)),
            full_spec((8, f)),
        ],
        out_shape=[
            jax.ShapeDtypeStruct((LEN, d), BF16),
            jax.ShapeDtypeStruct((LEN, f), BF16),
            jax.ShapeDtypeStruct((LEN, f), BF16),
            jax.ShapeDtypeStruct((LEN, d), BF16),
            jax.ShapeDtypeStruct((8, d), F32),
            jax.ShapeDtypeStruct((8, f), F32),
        ],
        name=f"mlp_bwd_{layer}",
    )(g, h, wfc, wproj)


def attn_bwd_kernel(layer, half, *refs):
    (g_i, own, oth, mid, qkv, att, lse, start, gain, wout) = refs[:10]
    (gm_o, low_o, dqkv_o, sums_o, qvs_o, k_t, dk, dv, dq_t) = refs[10:]
    g = pl.program_id(0)

    @pl.when(g == 0)
    def _():
        sums_o[...] = jnp.zeros_like(sums_o)
        qvs_o[...] = jnp.zeros_like(qvs_o)
        dk[...] = jnp.zeros_like(dk)
        dv[...] = jnp.zeros_like(dv)
        for b in range(LEN // BT):
            block = qkv[BT * b : BT * (b + 1), half : 2 * half].astype(F32)
            k_t[:, BT * b : BT * (b + 1)] = jnp.transpose(block).astype(BF16)

    gm, g_gain, g_shift = norm_back(
        g_i[...].astype(F32), own[...], oth[...], mid[...], gain[layer, 1:2, :].astype(F32)
    )
    gm_o[...] = gm
    sums_o[0:1, :] += colsum(g_gain)
    sums_o[1:2, :] += colsum(g_shift)
    sums_o[2:3, :] += colsum(gm)
    low = gm.astype(BF16)
    low_o[...] = low
    d_att = dot(low, wout[...], 1, 1).astype(BF16)
    prod = d_att.astype(F32) * att[...].astype(F32)
    head = lax.broadcasted_iota(jnp.int32, (8, half), 1) // HD
    pick = (head == lax.broadcasted_iota(jnp.int32, (8, half), 0)).astype(F32)
    inner = lax.dot_general(
        pick,
        prod,
        (((1,), (1,)), ((), ())),
        preferred_element_type=F32,
        precision=lax.Precision.HIGHEST,
    )
    rows = pl.ds(pl.multiple_of(g * BT, BT), BT)
    q = qkv[rows, :half] * jnp.asarray(1.0 / math.sqrt(HD), BF16)
    for s in range(BT // QB):
        i = g * (BT // QB) + s
        ks = pl.multiple_of(jnp.maximum(i - DOC_MOST // QB, 0) * QB, QB)
        bias = window_bias(start, i, ks)
        cols = pl.ds(pl.multiple_of(i * QB, QB), QB)
        win = pl.ds(ks, KW)
        for p in range(half // 128):
            lo = 128 * p
            qq = head_pair(q[QB * s : QB * (s + 1), lo : lo + 128])
            oo = head_pair(d_att[QB * s : QB * (s + 1), lo : lo + 128])
            kp = qkv[win, half + lo : half + lo + 128]
            vp = qkv[win, 2 * half + lo : 2 * half + lo + 128]
            total = jnp.concatenate(
                [lse[2 * p : 2 * p + 1, cols], lse[2 * p + 1 : 2 * p + 2, cols]], axis=1
            )
            inn = jnp.concatenate(
                [
                    inner[2 * p : 2 * p + 1, QB * s : QB * (s + 1)],
                    inner[2 * p + 1 : 2 * p + 2, QB * s : QB * (s + 1)],
                ],
                axis=1,
            )
            probs = jnp.exp(dot(kp, qq, 1, 1) + bias - total)
            d_probs = dot(vp, oo, 1, 1)
            ds = (probs * (d_probs - inn)).astype(BF16)
            dv[win, lo : lo + 128] += dot(probs.astype(BF16), oo)
            dk[win, lo : lo + 128] += dot(ds, qq)
            dqt = dot(k_t[lo : lo + 128, win], ds)
            dq_t[lo : lo + HD, :] = dqt[:HD, :QB]
            dq_t[lo + HD : lo + 128, :] = dqt[HD:, QB:]
        dq = (jnp.transpose(dq_t[...]) * (1.0 / math.sqrt(HD))).astype(BF16)
        dqkv_o[cols, :half] = dq
        qvs_o[0:1, :] += colsum(dq.astype(F32))

    @pl.when(g == pl.num_programs(0) - 1)
    def _():
        dqkv_o[:, half : 2 * half] = dk[...].astype(BF16)
        dvb = dv[...].astype(BF16)
        dqkv_o[:, 2 * half :] = dvb
        qvs_o[1:2, :] = colsum(dvb.astype(F32))


def attn_bwd(layer, g, own, oth, mid, qkv, att, lse, start, gain, wout):
    d = mid.shape[1]
    half = att.shape[1]
    ins = [g, own, oth, mid, qkv, att, lse, start, gain, wout]
    specs = [rows_spec(d)] * 4 + [full_spec(qkv.shape), rows_spec(half)]
    specs += [full_spec(a.shape) for a in ins[6:]]
    return pl.pallas_call(
        functools.partial(attn_bwd_kernel, layer, half),
        grid=(LEN // BT,),
        in_specs=specs,
        out_specs=[
            rows_spec(d),
            rows_spec(d),
            full_spec((LEN, 3 * half)),
            full_spec((8, d)),
            full_spec((8, half)),
        ],
        out_shape=[
            jax.ShapeDtypeStruct((LEN, d), F32),
            jax.ShapeDtypeStruct((LEN, d), BF16),
            jax.ShapeDtypeStruct((LEN, 3 * half), BF16),
            jax.ShapeDtypeStruct((8, d), F32),
            jax.ShapeDtypeStruct((8, half), F32),
        ],
        scratch_shapes=[
            pltpu.VMEM((half, LEN), BF16),
            pltpu.VMEM((LEN, half), F32),
            pltpu.VMEM((LEN, half), F32),
            pltpu.VMEM((half, QB), F32),
        ],
        name=f"attn_bwd_{layer}",
    )(*ins)


def norm_bwd_kernel(layer, g, own, oth, x, gain, g_o, sums_o):
    @pl.when(pl.program_id(0) == 0)
    def _():
        sums_o[...] = jnp.zeros_like(sums_o)

    out, g_gain, g_shift = norm_back(
        g[...], own[...], oth[...], x[...], gain[layer, 0:1, :].astype(F32)
    )
    g_o[...] = out
    sums_o[0:1, :] += colsum(g_gain)
    sums_o[1:2, :] += colsum(g_shift)


def norm_bwd(layer, g, own, oth, x, gain):
    d = x.shape[1]
    return pl.pallas_call(
        functools.partial(norm_bwd_kernel, layer),
        grid=(LEN // BT,),
        in_specs=[rows_spec(d)] * 4 + [full_spec(gain.shape)],
        out_specs=[rows_spec(d), full_spec((8, d))],
        out_shape=[jax.ShapeDtypeStruct((LEN, d), F32), jax.ShapeDtypeStruct((8, d), F32)],
        name=f"norm_bwd_{layer}",
    )(g, own, oth, x, gain)


def core_swap(a):
    return lax.ppermute(a, "mp", [(i, i ^ 1) for i in range(4)])


def y_swap(a):
    return lax.ppermute(a, "mp", [(i, i ^ 2) for i in range(4)])


def dp_swap(a, bit, n_dp):
    return lax.ppermute(a, "dp", [(i, i ^ (1 << bit)) for i in range(n_dp)])


def pick(flag, zero, one):
    return jnp.where(flag == 0, zero, one)


class Place:
    def __init__(self, n_dp):
        mp = lax.axis_index("mp")
        self.n_dp = n_dp
        self.bits = n_dp.bit_length() - 1
        self.y = mp // 2
        self.c = mp % 2
        self.dp = lax.axis_index("dp")

    def dp_bit(self, b):
        return (self.dp >> b) & 1


def gather_row(a, at):
    rows = a.reshape(2, LEN, a.shape[1])
    mine = pick(at.y, rows[0], rows[1])
    theirs = pick(at.y, rows[1], rows[0])
    far = y_swap(theirs)
    mine_c = core_swap(mine)
    far_c = core_swap(far)

    def joined(here, there):
        return [pick(at.c, here, there), pick(at.c, there, here)]

    near2, far2 = joined(mine, mine_c), joined(far, far_c)
    return jnp.concatenate(
        [pick(at.y, a_, b_) for a_, b_ in zip(near2, far2)]
        + [pick(at.y, b_, a_) for a_, b_ in zip(near2, far2)],
        axis=1,
    )


def own_cols(a, at, other):
    w = a.shape[1] // 4
    halves = (a[:, : 2 * w], a[:, 2 * w :])
    h = pick(at.y, halves[1], halves[0]) if other else pick(at.y, halves[0], halves[1])
    return pick(at.c, h[:, :w], h[:, w:])


def fetch(w, at):
    if at.n_dp == 1:
        return y_swap(w)
    r = w.shape[0] // 2
    b = at.dp_bit(0)
    a1 = y_swap(pick(b, w[:r], w[r:]))
    a2 = dp_swap(a1, 0, at.n_dp)
    return jnp.concatenate([pick(b, a1, a2), pick(b, a2, a1)], axis=0)


def scatter_sum(own, oth, order, at):
    d, width = own.shape
    k = at.bits
    lead = (2,) * k
    a = jnp.stack([own.astype(BF16), oth.astype(BF16)]).reshape(
        (2,) + lead + (d // at.n_dp, width)
    )
    left = ["y"] + [k - 1 - j for j in range(k)]
    order = [o for o in order if o in left] + [o for o in left if o not in order]
    for o in order:
        ax = left.index(o)
        zero = lax.index_in_dim(a, 0, ax, keepdims=False)
        one = lax.index_in_dim(a, 1, ax, keepdims=False)
        if o == "y":
            got = y_swap(one)
            keep = zero
        else:
            b = at.dp_bit(o)
            got = dp_swap(pick(b, one, zero), o, at.n_dp)
            keep = pick(b, zero, one)
        left.pop(ax)
        a = keep.astype(F32) + got.astype(F32)
        if left:
            a = a.astype(BF16)
    return a


def table_scatter(t, at, rows_all):
    a = t[0] + y_swap(t[1].astype(BF16)).astype(F32)
    if at.n_dp == 1:
        return jnp.pad(a, ((0, rows_all - a.shape[0]), (0, 0)))
    top = at.bits - 1
    half = rows_all // 2
    hi = [(i, i ^ (1 << top)) for i in range(at.n_dp) if i >> top & 1]
    a = a + lax.ppermute(a.astype(BF16), "dp", hi).astype(F32)
    a = pick(at.dp_bit(top), a, jnp.zeros_like(a))
    a = jnp.pad(a, ((0, half - a.shape[0]), (0, 0)))
    for b in range(top - 1, -1, -1):
        r = a.shape[0] // 2
        f = at.dp_bit(b)
        got = dp_swap(pick(f, a[r:], a[:r]).astype(BF16), b, at.n_dp)
        a = pick(f, a[:r], a[r:]) + got.astype(F32)
    return a


def small_scatter(shared, own, oth, at):
    n = at.n_dp
    got = y_swap(jnp.concatenate([shared, oth], axis=0))
    a = jnp.concatenate([shared, own], axis=0) + got
    r, d = a.shape
    a = a.reshape(r, n, d // n).transpose(1, 0, 2)
    for b in range(at.bits - 1, -1, -1):
        h = a.shape[0] // 2
        f = at.dp_bit(b)
        a = pick(f, a[:h], a[h:]) + dp_swap(pick(f, a[h:], a[:h]), b, n)
    return a[0]


def doc_positions(doc_ids):
    row_index = jnp.broadcast_to(jnp.arange(doc_ids.shape[1], dtype=jnp.int32), doc_ids.shape)
    previous = jnp.concatenate([doc_ids[:, :1] - 1, doc_ids[:, :-1]], axis=1)
    starts = jnp.where(doc_ids != previous, row_index, 0)
    return lax.cummax(starts, axis=1)


def tok_dot(a, b):
    return lax.dot_general(a, b, (((0,), (0,)), ((), ())), preferred_element_type=F32).astype(BF16)


def on_device(
    n_dp,
    tokens,
    doc_ids,
    positions_table,
    norm_gain,
    norm_shift,
    joined_projection_weight,
    qv_bias,
    w_out,
    out_bias,
    w_fc,
    fc_bias,
    w_proj,
    cotangent,
):
    at = Place(n_dp)
    d = positions_table.shape[1]
    share = joined_projection_weight.shape[-1]
    layers = w_fc.shape[0]

    starts = doc_positions(doc_ids)
    start = pick(at.y, starts[0:1], starts[1:2])
    place = jnp.arange(LEN, dtype=jnp.int32) - start[0]
    hot = (place[:, None] == jnp.arange(DOC_MOST, dtype=jnp.int32)[None, :]).astype(BF16)
    embedded = lax.dot_general(
        hot, positions_table[:DOC_MOST], (((1,), (0,)), ((), ())), preferred_element_type=F32
    ).astype(BF16)
    full_tokens = gather_row(tokens, at)

    small = jnp.concatenate([qv_bias.reshape(-1), fc_bias.reshape(-1)])
    small_o = y_swap(small)
    nq = qv_bias.size
    qvb = jnp.concatenate([qv_bias, small_o[:nq].reshape(qv_bias.shape)], axis=-1)
    fcb = jnp.concatenate([fc_bias, small_o[nq:].reshape(fc_bias.shape)], axis=-1)

    wqkv, wout, wfc, wproj = [], [], [], []
    for l in range(layers):
        own = joined_projection_weight[l]
        flat = own.reshape(d, 3 * share)
        oth = fetch(flat, at).reshape(own.shape)
        wqkv.append(jnp.concatenate([own, oth], axis=-1).reshape(d, 6 * share))
        wout.append(jnp.concatenate([w_out[l], fetch(w_out[l], at)], axis=0))
        wfc.append(jnp.concatenate([w_fc[l], fetch(w_fc[l], at)], axis=1))
        wproj.append(jnp.concatenate([w_proj[l], fetch(w_proj[l], at)], axis=0))

    kept = []
    stream_in = (full_tokens, embedded)
    for l in range(layers):
        x, normed, qkv, att, lse, part = attn_fwd(
            l, stream_in, start, norm_gain, norm_shift, wqkv[l], qvb, wout[l], out_bias
        )
        mid, normed2, hidden, part2 = mlp_fwd(
            l, x, part, core_swap(part), out_bias, norm_gain, norm_shift, wfc[l], fcb, wproj[l]
        )
        stream_in = (mid, part2, core_swap(part2))
        kept.append((x, normed, qkv, att, lse, mid, normed2, hidden))

    result = (
        stream_in[0]
        + (stream_in[1].astype(F32) + stream_in[2].astype(F32))
        + out_bias[layers - 1, 1].astype(F32)
    ).astype(BF16)
    out_far = y_swap(own_cols(result, at, True))
    out_near = own_cols(result, at, False)
    out = jnp.concatenate([pick(at.y, out_near, out_far), pick(at.y, out_far, out_near)], axis=0)

    g = gather_row(cotangent, at)
    grads = [None] * layers
    for l in range(layers - 1, -1, -1):
        x, normed, qkv, att, lse, mid, normed2, hidden = kept[l]
        g_low, act, g_hid, part, sum_g, sum_h = mlp_bwd(l, g, hidden, wfc[l], wproj[l])
        far = core_swap(part)
        d_fc = tok_dot(normed2, g_hid)
        d_proj = tok_dot(g_low, act)
        gm, m_low, dqkv, sums2, qvs = attn_bwd(
            l, g, part, far, mid, qkv, att, lse, start, norm_gain, wout[l]
        )
        part = lax.dot_general(
            dqkv, wqkv[l], (((1,), (1,)), ((), ())), preferred_element_type=F32
        ).astype(BF16)
        far = core_swap(part)
        d_out = tok_dot(m_low, att)
        d_qkv = tok_dot(normed, dqkv)
        g, sums1 = norm_bwd(l, gm, part, far, x, norm_gain)
        f = w_fc.shape[-1]
        q6 = d_qkv.reshape(d, 3, 2, share)
        ao_own = jnp.concatenate([q6[:, j, 0] for j in range(3)] + [d_out[:, :share]], axis=1)
        ao_oth = jnp.concatenate([q6[:, j, 1] for j in range(3)] + [d_out[:, share:]], axis=1)
        r_fc = scatter_sum(d_fc[:, :f], d_fc[:, f:], ["y", 0, 1, 2], at)
        r_proj = scatter_sum(d_proj[:, :f], d_proj[:, f:], [0, 1, "y", 2], at)
        r_ao = scatter_sum(ao_own, ao_oth, [1, "y", 0, 2], at)
        grads[l] = (r_fc, r_proj, r_ao, sums1, sums2, sum_g, sum_h, qvs)

    near = own_cols(g, at, False)
    far_send = own_cols(g, at, True).astype(BF16)
    far = y_swap(far_send).astype(F32)
    grad_tokens = jnp.concatenate([pick(at.y, near, far), pick(at.y, far, near)], axis=0)
    table = lax.dot_general(
        hot,
        jnp.concatenate([near.astype(BF16), far_send], axis=1),
        (((0,), (0,)), ((), ())),
        preferred_element_type=F32,
    )
    grad_positions = table_scatter(
        jnp.stack([table[:, :share], table[:, share:]]), at, positions_table.shape[0]
    )

    def qv_row(qvs, lo):
        parts = jnp.stack([q[j, lo : lo + share] for q in qvs for j in range(2)])
        return parts.reshape(-1, n_dp, share // n_dp).transpose(1, 0, 2).reshape(1, d)

    f = w_fc.shape[-1]
    shared = jnp.stack(
        [grads[l][3][0] if w == 0 else grads[l][4][0] for l in range(layers) for w in range(2)]
        + [grads[l][3][1] if w == 0 else grads[l][4][1] for l in range(layers) for w in range(2)]
        + [grads[l][4][2] if w == 0 else grads[l][5][0] for l in range(layers) for w in range(2)]
    )
    qvs = [grads[l][7] for l in range(layers)]
    own = jnp.concatenate([jnp.stack([grads[l][6][0, :f] for l in range(layers)]), qv_row(qvs, 0)])
    oth = jnp.concatenate(
        [jnp.stack([grads[l][6][0, f:] for l in range(layers)]), qv_row(qvs, share)]
    )
    s = small_scatter(shared, own, oth, at)
    w = d // n_dp
    ao = jnp.stack([grads[l][2] for l in range(layers)])
    return (
        out,
        grad_tokens,
        grad_positions,
        s[0:4].reshape(2, 2, w),
        s[4:8].reshape(2, 2, w),
        ao[..., : 3 * share].reshape(layers, w, 3, share),
        s[14].reshape(2, 2, w // 4),
        jnp.swapaxes(ao[..., 3 * share :], 1, 2),
        s[8:12].reshape(2, 2, w),
        jnp.stack([grads[l][0] for l in range(layers)]),
        s[12:14],
        jnp.stack([grads[l][1].T for l in range(layers)]),
    )


def solution(mesh):
    n_dp = mesh.shape["dp"]
    in_specs = (
        P("dp", "mp"),
        P("dp", None),
        P(),
        P(),
        P(),
        P(None, None, None, "mp"),
        P(None, None, "mp"),
        P(None, "mp", None),
        P(),
        P(None, None, "mp"),
        P(None, "mp"),
        P(None, "mp", None),
        P("dp", "mp"),
    )
    out_specs = (
        P("dp", "mp"),
        P("dp", "mp"),
        P("dp", "mp"),
        P(None, None, "dp"),
        P(None, None, "dp"),
        P(None, "dp", None, "mp"),
        P(None, None, ("mp", "dp")),
        P(None, "mp", "dp"),
        P(None, None, "dp"),
        P(None, "dp", "mp"),
        P(None, ("mp", "dp")),
        P(None, "mp", "dp"),
    )
    return jax.shard_map(
        functools.partial(on_device, n_dp),
        mesh=mesh,
        in_specs=in_specs,
        out_specs=out_specs,
        check_vma=False,
    )
```

time: 1660 us -> 647 us (0.39)
  waiting for transfers between devices: 1030 us -> 216 us
  matrix products: 234 us -> 41.6 us
  Pallas kernels: 0 us -> 141 us
  other arithmetic: 212 us -> 80.2 us
  starting transfers between devices: 1.93 us -> 62.4 us
  local copies, waits for them, and re-layouts: 136 us -> 91.6 us
  blocking collectives: 19.4 us -> 0 us
    psum x7 -> x0, waiting for transfers between devices: 441 us -> none  [the longest x2 135 us: block_forward(): lax.psum(jnp.dot(attended, w_out, preferred_element_type=jnp.float32).ast...]
    unnamed x25 -> x0, waiting for transfers between devices: 426 us -> none
    ppermute x0 -> x65, waiting for transfers between devices: none -> 216 us  [the longest x31 125 us: dp_swap(): return lax.ppermute(a, 'dp', [(i, i ^ 1 << bit) for i in range(n_dp)])]
    dot_general x50 -> x12, matrix products: 224 us -> 41.6 us  [the longest x8 28.8 us: tok_dot(): lax.dot_general(a, b, (((0,), (0,)), ((), ())), preferred_element_type=F32)]
    pallas_call x0 -> x10, Pallas kernels: none -> 141 us  [the longest x2 41 us: attn_fwd(): pl.pallas_call(functools.partial(attn_fwd_kernel, layer, first, half), gr...]
    reduce_sum x32 -> x0, other arithmetic: 125 us -> none  [the longest x11 47.9 us: layer_norm(): return centred * lax.rsqrt(variance + epsilon) * gain_row + shift_row]
    reduce_scatter x2 -> x0, waiting for transfers between devices: 125 us -> none  [the longest x1 62.7 us: on_device(): lax.psum_scatter(merged_result[6].astype(jnp.bfloat16), 'dp', scatter_dim...]
    ppermute x0 -> x65, starting transfers between devices: none -> 62.4 us  [the longest x31 36.2 us: dp_swap(): return lax.ppermute(a, 'dp', [(i, i ^ 1 << bit) for i in range(n_dp)])]
  transfers between devices with their start and end apart: 18 -> 65, of which waited for: 18 -> 27; matrix products, arithmetic and copies ran while one was open for 11% -> 31% of each run, Pallas kernels for 0% -> 17%
where the time goes in v1:
time: 647 us; the launch traced here: 635 us
  waiting for transfers between devices  216 us (33%)
  Pallas kernels  141 us (22%)
  local copies, waits for them, and re-layouts  91.6 us (14%)
  other arithmetic  80.2 us (12%)
  starting transfers between devices  62.4 us (10%)
  matrix products  41.6 us (6%)
    ppermute x31, waiting for transfers between devices, dp_swap(): return lax.ppermute(a, 'dp', [(i, i ^ 1 << bit) for i in range(n_dp)])  125 us
    ppermute x21, waiting for transfers between devices, y_swap(): return lax.ppermute(a, 'mp', [(i, i ^ 2) for i in range(4)])  85.3 us
    pallas_call x2, Pallas kernels, attn_fwd(): pl.pallas_call(functools.partial(attn_fwd_kernel, layer, first, half), gr...  41 us
    pallas_call x2, Pallas kernels, attn_bwd(): pl.pallas_call(functools.partial(attn_bwd_kernel, layer, half), grid=(LEN...  40.2 us
    ppermute x31, starting transfers between devices, dp_swap(): return lax.ppermute(a, 'dp', [(i, i ^ 1 << bit) for i in range(n_dp)])  36.2 us
    select_n x43, other arithmetic, pick(): return jnp.where(flag == 0, zero, one)  31.2 us
    dot_general x8, matrix products, tok_dot(): lax.dot_general(a, b, (((0,), (0,)), ((), ())), preferred_element_type=F32)  28.8 us
    pallas_call x2, Pallas kernels, mlp_bwd(): pl.pallas_call(mlp_bwd_kernel, grid=(LEN // BT,), in_specs=[rows_spec(d),...  23.8 us
  transfers between devices with their start and end apart: 65, of which 27 were waited for; matrix products, arithmetic and copies ran while one was open for 31% of the time, Pallas kernels for 17%

profile of v1, /device:TPU:0, one launch (start us, length us, event | category | flops | bytes accessed | tf_op | source)
XLA Modules:
  0.0 635.5 jit_solution(12317003057842336381)
XLA Ops:
  2.1 3.1 collective-permute-start.5
  17.7 2.7 select_bitcast_fusion.8
  21.7 3.2 convolution_convert_fusion.8.refs_1_
  29.5 3.6 collective-permute-done.7
  37.5 23.8 %collective-permute-done.3 = bf16[384,576]{0,1:T(8,128)(2,1)S(1)} collective-permute-done((bf16[384,576]{0,1:T(8,128)(2,1)S(1)}, bf16[384,576]{0,1:T(8,128)(2,1)S(1)}, u32[]{:S(2)}, u32[]{:S(2)}) %collective-permute-start.3) | collective-permute-done | bytes 442400 | tf_op jit(solution)/shard_map/ppermute | solution.py:406
  63.3 6.1 collective-permute-done.14
  76.5 5.9 collective-permute-done.15
  84.8 2.5 copy.253.refs_5_
  87.4 20.1 %attn_fwd_0.1 = (f32[1024,768]{1,0:T(8,128)}, bf16[1024,768]{1,0:T(8,128)(2,1)}, bf16[1024,1152]{1,0:T(8,128)(2,1)}, bf16[1024,384]{1,0:T(8,128)(2,1)}, f32[8,1024]{1,0:T(8,128)}, /*index=5*/bf16[1024,768]{1,0:T(8,128)(2,1)}) custom-call(bf16[1024,768]{1,0:T(8,128)(2,1)} %pad_maximum_fusion.5.refs_0_, bf16[1024,768]{1,0:T(8,128)(2,1)} %convolution_convert_fusion.8.refs_1_, ...), custom_call_target="tpu_custom_call" | custom-call | tf_op jit(solution)/shard_map/attn_fwd_0/pallas_call | solution.py:148
  115.3 11.4 %mlp_fwd_0.1 = (f32[1024,768]{1,0:T(8,128)}, bf16[1024,768]{1,0:T(8,128)(2,1)}, bf16[1024,1536]{1,0:T(8,128)(2,1)}, bf16[1024,768]{1,0:T(8,128)(2,1)}) custom-call(f32[1024,768]{1,0:T(8,128)} %get-tuple-element.58.x, bf16[1024,768]{1,0:T(8,128)(2,1)} %get-tuple-element.59.own, bf16[1024,768]{1,0:T(8,128)(2,1)} %collective-permute-done.8.oth, ...), custom_call_target="tpu_custom_call" | custom-call | tf_op jit(solution)/shard_map/mlp_fwd_0/pallas_call | solution.py:197
  135.9 3.7 collective-permute-done.17
  140.6 29.2 %collective-permute-done.26 = bf16[1024,192]{1,0:T(8,128)(2,1)} collective-permute-done((bf16[1024,192]{1,0:T(8,128)(2,1)S(1)}, bf16[1024,192]{1,0:T(8,128)(2,1)}, u32[]{:S(2)}, u32[]{:S(2)}) %collective-permute-start.26) | collective-permute-done | bytes 393248 | tf_op jit(solution)/shard_map/ppermute | solution.py:406
  175.2 20.9 %attn_fwd_1.1 = (f32[1024,768]{1,0:T(8,128)}, bf16[1024,768]{1,0:T(8,128)(2,1)}, bf16[1024,1152]{1,0:T(8,128)(2,1)}, bf16[1024,384]{1,0:T(8,128)(2,1)}, f32[8,1024]{1,0:T(8,128)}, /*index=5*/bf16[1024,768]{1,0:T(8,128)(2,1)}) custom-call(f32[1024,768]{1,0:T(8,128)} %get-tuple-element.60.refs_0_.refs_3_, bf16[1024,768]{1,0:T(8,128)(2,1)} %get-tuple-element.61.refs_1_, ...), custom_call_target="tpu_custom_call" | custom-call | tf_op jit(solution)/shard_map/attn_fwd_1/pallas_call | solution.py:148
  205.5 11.3 %mlp_fwd_1.1 = (f32[1024,768]{1,0:T(8,128)}, bf16[1024,768]{1,0:T(8,128)(2,1)}, bf16[1024,1536]{1,0:T(8,128)(2,1)}, bf16[1024,768]{1,0:T(8,128)(2,1)}) custom-call(f32[1024,768]{1,0:T(8,128)} %get-tuple-element.62.x, bf16[1024,768]{1,0:T(8,128)(2,1)} %get-tuple-element.63.own, bf16[1024,768]{1,0:T(8,128)(2,1)} %collective-permute-done.18.oth, ...), custom_call_target="tpu_custom_call" | custom-call | tf_op jit(solution)/shard_map/mlp_fwd_1/pallas_call | solution.py:197
  216.8 11.6 %mlp_bwd_1.1 = (bf16[1024,768]{1,0:T(8,128)(2,1)}, bf16[1024,1536]{1,0:T(8,128)(2,1)}, bf16[1024,1536]{1,0:T(8,128)(2,1)}, bf16[1024,768]{1,0:T(8,128)(2,1)}, f32[8,768]{1,0:T(8,128)}, /*index=5*/f32[8,1536]{1,0:T(8,128)}) custom-call(bf16[1024,768]{1,0:T(8,128)(2,1)} %pad_maximum_fusion.6.g.refs_0_, bf16[1024,1536]{1,0:T(8,128)(2,1)} %get-tuple-element.66.h, ...), custom_call_target="tpu_custom_call" | custom-call | tf_op jit(solution)/shard_map/mlp_bwd_1/pallas_call | solution.py:239
  228.5 5.0 convolution_convert_fusion.2
  236.4 3.1 convolution_convert_fusion
  247.2 16.2 %collective-permute-done.53 = bf16[2,2,2,96,768]{4,3,2,1,0:T(8,128)(2,1)} collective-permute-done((bf16[2,2,2,96,768]{4,3,2,1,0:T(8,128)(2,1)}, bf16[2,2,2,96,768]{4,3,2,1,0:T(8,128)(2,1)}, u32[]{:S(2)}, u32[]{:S(2)}) %collective-permute-start.53) | collective-permute-done | bytes 1179680 | tf_op jit(solution)/shard_map/ppermute | solution.py:406
  267.5 4.0 collective-permute-done.61
  277.0 2.5 add_convert_fusion
  283.1 19.9 %attn_bwd_1.1 = (f32[1024,768]{1,0:T(8,128)}, bf16[1024,768]{1,0:T(8,128)(2,1)}, bf16[1024,1152]{1,0:T(8,128)(2,1)}, f32[8,768]{1,0:T(8,128)}, f32[8,384]{1,0:T(8,128)}) custom-call(bf16[1024,768]{1,0:T(8,128)(2,1)} %pad_maximum_fusion.6.g.refs_0_, bf16[1024,768]{1,0:T(8,128)(2,1)} %get-tuple-element.67.refs_1_, ...), custom_call_target="tpu_custom_call" | custom-call | tf_op jit(solution)/shard_map/attn_bwd_1/pallas_call | solution.py:348
  303.0 5.3 convolution_convert_fusion.7.own
  311.7 4.4 convolution_convert_fusion.4
  328.7 3.2 maximum_maximum_fusion.3
  346.7 21.9 %collective-permute-done.55 = bf16[2,96,768]{2,1,0:T(8,128)(2,1)} collective-permute-done((bf16[2,96,768]{2,1,0:T(8,128)(2,1)}, bf16[2,96,768]{2,1,0:T(8,128)(2,1)}, u32[]{:S(2)}, u32[]{:S(2)}) %collective-permute-start.55) | collective-permute-done | bytes 294944 | tf_op jit(solution)/shard_map/ppermute | solution.py:410
  369.6 2.7 collective-permute-start.56
  373.8 8.2 %collective-permute-done.56 = bf16[96,768]{1,0:T(8,128)(2,1)S(1)} collective-permute-done((bf16[96,768]{1,0:T(8,128)(2,1)S(1)}, bf16[96,768]{1,0:T(8,128)(2,1)S(1)}, u32[]{:S(2)}, u32[]{:S(2)}) %collective-permute-start.56) | collective-permute-done | bytes 147488 | tf_op jit(solution)/shard_map/ppermute | solution.py:410
  386.6 6.8 %norm_bwd_1.1 = (f32[1024,768]{1,0:T(8,128)}, f32[8,768]{1,0:T(8,128)}) custom-call(f32[1024,768]{1,0:T(8,128)} %get-tuple-element.71.g, bf16[1024,768]{1,0:T(8,128)(2,1)} %convolution_convert_fusion.7.own, bf16[1024,768]{1,0:T(8,128)(2,1)} %collective-permute-done.29.oth, f32[1024,768]{1,0:T(8,128)} %get-tuple-element.62.x, bf16[2,2,768]{2,1,0:T(2,128)(2,1)} %gain.7), custom_call_target="tpu_custom_call" | custom-call | tf_op jit(solution)/shard_map/norm_bwd_1/pallas_call | solution.py:391
  393.3 12.2 %mlp_bwd_0.1 = (bf16[1024,768]{1,0:T(8,128)(2,1)}, bf16[1024,1536]{1,0:T(8,128)(2,1)}, bf16[1024,1536]{1,0:T(8,128)(2,1)}, bf16[1024,768]{1,0:T(8,128)(2,1)}, f32[8,768]{1,0:T(8,128)}, /*index=5*/f32[8,1536]{1,0:T(8,128)}) custom-call(f32[1024,768]{1,0:T(8,128)} %get-tuple-element.73.g.refs_0_, bf16[1024,1536]{1,0:T(8,128)(2,1)} %get-tuple-element.74.h, ...), custom_call_target="tpu_custom_call" | custom-call | tf_op jit(solution)/shard_map/mlp_bwd_0/pallas_call | solution.py:239
  406.8 5.1 convolution_convert_fusion.3
  414.3 2.9 convolution_convert_fusion.1
  421.6 6.2 collective-permute-done.47
  429.4 6.4 %collective-permute-done.48 = bf16[96,768]{1,0:T(8,128)(2,1)S(1)} collective-permute-done((bf16[96,768]{1,0:T(8,128)(2,1)S(1)}, bf16[96,768]{1,0:T(8,128)(2,1)S(1)}, u32[]{:S(2)}, u32[]{:S(2)}) %collective-permute-start.48) | collective-permute-done | bytes 147488 | tf_op jit(solution)/shard_map/ppermute | solution.py:410
  441.1 11.9 %collective-permute-done.57 = bf16[2,2,2,96,768]{4,3,2,1,0:T(8,128)(2,1)S(1)} collective-permute-done((bf16[2,2,2,96,768]{4,3,2,1,0:T(8,128)(2,1)S(1)}, bf16[2,2,2,96,768]{4,3,2,1,0:T(8,128)(2,1)S(1)}, u32[]{:S(2)}, u32[]{:S(2)}) %collective-permute-start.57) | collective-permute-done | bytes 1179680 | tf_op jit(solution)/shard_map/ppermute | solution.py:410
  456.6 20.4 %attn_bwd_0.1 = (f32[1024,768]{1,0:T(8,128)}, bf16[1024,768]{1,0:T(8,128)(2,1)}, bf16[1024,1152]{1,0:T(8,128)(2,1)}, f32[8,768]{1,0:T(8,128)}, f32[8,384]{1,0:T(8,128)}) custom-call(f32[1024,768]{1,0:T(8,128)} %get-tuple-element.73.g.refs_0_, bf16[1024,768]{1,0:T(8,128)(2,1)} %get-tuple-element.75.refs_1_, bf16[1024,768]{1,0:T(8,128)(2,1)} %copy-done.32, ...), custom_call_target="tpu_custom_call" | custom-call | tf_op jit(solution)/shard_map/attn_bwd_0/pallas_call | solution.py:348
  484.8 5.1 convolution_convert_fusion.5
  489.9 2.6 copy.260
  507.9 3.5 maximum_maximum_fusion.2
  513.3 3.3 convolution_convert_fusion.6.own
  527.8 25.7 %collective-permute-done.51 = bf16[2,96,768]{2,1,0:T(8,128)(2,1)S(1)} collective-permute-done((bf16[2,96,768]{2,1,0:T(8,128)(2,1)S(1)}, bf16[2,96,768]{2,1,0:T(8,128)(2,1)S(1)}, u32[]{:S(2)}, u32[]{:S(2)}) %collective-permute-start.51) | collective-permute-done | bytes 294944 | tf_op jit(solution)/shard_map/ppermute | solution.py:410
  553.7 2.7 collective-permute-start.52
  556.8 8.3 %collective-permute-done.52 = bf16[96,768]{1,0:T(8,128)(2,1)S(1)} collective-permute-done((bf16[96,768]{1,0:T(8,128)(2,1)S(1)}, bf16[96,768]{1,0:T(8,128)(2,1)S(1)}, u32[]{:S(2)}, u32[]{:S(2)}) %collective-permute-start.52) | collective-permute-done | bytes 147488 | tf_op jit(solution)/shard_map/ppermute | solution.py:410
  572.0 6.8 %norm_bwd_0.1 = (f32[1024,768]{1,0:T(8,128)}, f32[8,768]{1,0:T(8,128)}) custom-call(f32[1024,768]{1,0:T(8,128)} %get-tuple-element.79.g, bf16[1024,768]{1,0:T(8,128)(2,1)} %convolution_convert_fusion.6.own, bf16[1024,768]{1,0:T(8,128)(2,1)} %copy-done.33, f32[1024,768]{1,0:T(8,128)} %get-tuple-element.58.x, bf16[2,2,768]{2,1,0:T(2,128)(2,1)} %gain.7), custom_call_target="tpu_custom_call" | custom-call | tf_op jit(solution)/shard_map/norm_bwd_0/pallas_call | solution.py:391
  586.6 4.7 collective-permute-done.38
  591.9 3.2 collective-permute-done.39
  600.7 5.1 collective-permute-done.33
  608.4 5.8 collective-permute-done.34
  626.4 6.4 %collective-permute-done.44 = bf16[96,768]{1,0:T(8,128)(2,1)S(1)} collective-permute-done((bf16[96,768]{1,0:T(8,128)(2,1)S(1)}, bf16[96,768]{1,0:T(8,128)(2,1)S(1)}, u32[]{:S(2)}, u32[]{:S(2)}) %collective-permute-start.44) | collective-permute-done | bytes 147488 | tf_op jit(solution)/shard_map/ppermute | solution.py:410
  (473 shorter events, 222.6 us)
Async XLA Ops:
  2.1 22.9 %collective-permute-start.5 = (bf16[2304]{0:T(1024)(128)(2,1)S(1)}, bf16[2304]{0:T(1024)(128)(2,1)S(1)}, u32[]{:S(2)}, u32[]{:S(2)}) collective-permute-start(bf16[2304]{0:T(1024)(128)(2,1)S(1)} %pad_maximum_fusion.17), channel_id=1, source_target_pairs={{0,2},{1,3},{2,0},{3,1},{4,6},{5,7},{6,4},{7,5},{8,10},{9,11},{10,... | collective-permute-start | bytes 13832 | tf_op jit(solution)/shard_map/ppermute | solution.py:406
  7.0 20.1 %collective-permute-start.6 = (bf16[96,768]{1,0:T(8,128)(2,1)}, bf16[96,768]{1,0:T(8,128)(2,1)}, u32[]{:S(2)}, u32[]{:S(2)}) collective-permute-start(bf16[96,768]{1,0:T(8,128)(2,1)} %get-tuple-element.257), channel_id=1, source_target_pairs={{0,2},{1,3},{2,0},{3,1},{4,6},{5,7},{6,4},{7,5},{8,10},{9,11},{10,... | collective-permute-start | bytes 442376 | tf_op jit(solution)/shard_map/ppermute | solution.py:406
  11.5 21.8 %collective-permute-start.1 = (bf16[1024,192]{1,0:T(8,128)(2,1)}, bf16[1024,192]{1,0:T(8,128)(2,1)}, u32[]{:S(2)}, u32[]{:S(2)}) collective-permute-start(bf16[1024,192]{1,0:T(8,128)(2,1)} %get-tuple-element.240), channel_id=1, source_target_pairs={{0,2},{1,3},{2,0},{3,1},{4,6},{5,7},{6,4},{7,5},{8,10},{9,11},{10,... | collective-permute-start | bytes 1179656 | tf_op jit(solution)/shard_map/ppermute | solution.py:406
  13.5 21.5 %collective-permute-start = (bf16[1024,192]{1,0:T(8,128)(2,1)}, bf16[1024,192]{1,0:T(8,128)(2,1)}, u32[]{:S(2)}, u32[]{:S(2)}) collective-permute-start(bf16[1024,192]{1,0:T(8,128)(2,1)} %get-tuple-element.241), channel_id=1, source_target_pairs={{0,1},{1,0},{2,3},{3,2},{4,5},{5,4},{6,7},{7,6},{8,9},{9,8},{10,11... | collective-permute-start | bytes 1179656 | tf_op jit(solution)/shard_map/ppermute | solution.py:402
  14.7 56.4 %collective-permute-start.9 = (bf16[384,768]{1,0:T(8,128)(2,1)}, bf16[384,768]{1,0:T(8,128)(2,1)}, u32[]{:S(2)}, u32[]{:S(2)}) collective-permute-start(bf16[384,768]{1,0:T(8,128)(2,1)} %get-tuple-element.199), channel_id=1, source_target_pairs={{0,2},{1,3},{2,0},{3,1},{4,6},{5,7},{6,4},{7,5},{8,10},{9,11},{10,... | collective-permute-start | bytes 1769480 | tf_op jit(solution)/shard_map/ppermute | solution.py:406
  25.0 46.4 %collective-permute-start.11 = (bf16[384,768]{1,0:T(8,128)(2,1)S(1)}, bf16[384,768]{1,0:T(8,128)(2,1)}, u32[]{:S(2)}, u32[]{:S(2)}) collective-permute-start(bf16[384,768]{1,0:T(8,128)(2,1)S(1)} %get-tuple-element.195), channel_id=1, source_target_pairs={{0,2},{1,3},{2,0},{3,1},{4,6},{5,7},{6,4},{7,5},{8,10},{9,11},{10,... | collective-permute-start | bytes 1769480 | tf_op jit(solution)/shard_map/ppermute | solution.py:406
  33.0 28.3 %collective-permute-start.3 = (bf16[384,576]{0,1:T(8,128)(2,1)S(1)}, bf16[384,576]{0,1:T(8,128)(2,1)S(1)}, u32[]{:S(2)}, u32[]{:S(2)}) collective-permute-start(bf16[384,576]{0,1:T(8,128)(2,1)S(1)} %bitcast.318), channel_id=1, source_target_pairs={{0,2},{1,3},{2,0},{3,1},{4,6},{5,7},{6,4},{7,5},{8,10},{9,11},{10,... | collective-permute-start | bytes 1327112 | tf_op jit(solution)/shard_map/ppermute | solution.py:406
  33.4 36.0 %collective-permute-start.14 = (bf16[384,576]{0,1:T(8,128)(2,1)S(1)}, bf16[384,576]{0,1:T(8,128)(2,1)S(1)}, u32[]{:S(2)}, u32[]{:S(2)}) collective-permute-start(bf16[384,576]{0,1:T(8,128)(2,1)S(1)} %bitcast.317), channel_id=1, source_target_pairs={{0,2},{1,3},{2,0},{3,1},{4,6},{5,7},{6,4},{7,5},{8,10},{9,11},{10,... | collective-permute-start | bytes 1327112 | tf_op jit(solution)/shard_map/ppermute | solution.py:406
  35.1 38.1 %collective-permute-start.2 = (bf16[1024,192]{1,0:T(8,128)(2,1)}, bf16[1024,192]{1,0:T(8,128)(2,1)S(1)}, u32[]{:S(2)}, u32[]{:S(2)}) collective-permute-start(bf16[1024,192]{1,0:T(8,128)(2,1)} %collective-permute-done.1), channel_id=1, source_target_pairs={{0,1},{1,0},{2,3},{3,2},{4,5},{5,4},{6,7},{7,6},{8,9},{9,8},{10,11... | collective-permute-start | bytes 1179656 | tf_op jit(solution)/shard_map/ppermute | solution.py:402
  61.3 15.2 %collective-permute-start.4 = (bf16[384,576]{0,1:T(8,128)(2,1)S(1)}, bf16[384,576]{0,1:T(8,128)(2,1)S(1)}, u32[]{:S(2)}, u32[]{:S(2)}) collective-permute-start(bf16[384,576]{0,1:T(8,128)(2,1)S(1)} %collective-permute-done.3), channel_id=1, source_target_pairs={{0,4},{4,0},{8,12},{12,8},{16,20},{20,16},{24,28},{28,24},{1,5},{5... | collective-permute-start | bytes 1327112 | tf_op jit(solution)/shard_map/ppermute | solution.py:410
  69.4 13.0 %collective-permute-start.15 = (bf16[384,576]{0,1:T(8,128)(2,1)S(1)}, bf16[384,576]{0,1:T(8,128)(2,1)S(1)}, u32[]{:S(2)}, u32[]{:S(2)}) collective-permute-start(bf16[384,576]{0,1:T(8,128)(2,1)S(1)} %collective-permute-done.14), channel_id=1, source_target_pairs={{0,4},{4,0},{8,12},{12,8},{16,20},{20,16},{24,28},{28,24},{1,5},{5... | collective-permute-start | bytes 1327112 | tf_op jit(solution)/shard_map/ppermute | solution.py:410
  71.1 38.1 %collective-permute-start.10 = (bf16[384,768]{1,0:T(8,128)(2,1)}, bf16[384,768]{1,0:T(8,128)(2,1)}, u32[]{:S(2)}, u32[]{:S(2)}) collective-permute-start(bf16[384,768]{1,0:T(8,128)(2,1)} %collective-permute-done.9), channel_id=1, source_target_pairs={{0,4},{4,0},{8,12},{12,8},{16,20},{20,16},{24,28},{28,24},{1,5},{5... | collective-permute-start | bytes 1769480 | tf_op jit(solution)/shard_map/ppermute | solution.py:410
  71.4 39.1 %collective-permute-start.12 = (bf16[384,768]{1,0:T(8,128)(2,1)}, bf16[384,768]{1,0:T(8,128)(2,1)}, u32[]{:S(2)}, u32[]{:S(2)}) collective-permute-start(bf16[384,768]{1,0:T(8,128)(2,1)} %collective-permute-done.11), channel_id=1, source_target_pairs={{0,4},{4,0},{8,12},{12,8},{16,20},{20,16},{24,28},{28,24},{1,5},{5... | collective-permute-start | bytes 1769480 | tf_op jit(solution)/shard_map/ppermute | solution.py:410
  126.7 48.5 %collective-permute-start.13 = (bf16[1024,768]{1,0:T(8,128)(2,1)}, bf16[1024,768]{1,0:T(8,128)(2,1)}, u32[]{:S(2)}, u32[]{:S(2)}) collective-permute-start(bf16[1024,768]{1,0:T(8,128)(2,1)} %get-tuple-element.61.refs_1_), channel_id=1, source_target_pairs={{0,1},{1,0},{2,3},{3,2},{4,5},{5,4},{6,7},{7,6},{8,9},{9,8},{10,11... | collective-permute-start | bytes 4718600 | tf_op jit(solution)/shard_map/ppermute | solution.py:402
  128.9 41.8 %collective-permute-start.19 = (bf16[384,768]{1,0:T(8,128)(2,1)}, bf16[384,768]{1,0:T(8,128)(2,1)}, u32[]{:S(2)}, u32[]{:S(2)}) collective-permute-start(bf16[384,768]{1,0:T(8,128)(2,1)} %get-tuple-element.198), channel_id=1, source_target_pairs={{0,2},{1,3},{2,0},{3,1},{4,6},{5,7},{6,4},{7,5},{8,10},{9,11},{10,... | collective-permute-start | bytes 1769480 | tf_op jit(solution)/shard_map/ppermute | solution.py:406
  129.2 43.2 %collective-permute-start.21 = (bf16[384,768]{1,0:T(8,128)(2,1)}, bf16[384,768]{1,0:T(8,128)(2,1)}, u32[]{:S(2)}, u32[]{:S(2)}) collective-permute-start(bf16[384,768]{1,0:T(8,128)(2,1)} %get-tuple-element.194), channel_id=1, source_target_pairs={{0,2},{1,3},{2,0},{3,1},{4,6},{5,7},{6,4},{7,5},{8,10},{9,11},{10,... | collective-permute-start | bytes 1769480 | tf_op jit(solution)/shard_map/ppermute | solution.py:406
  131.5 38.3 %collective-permute-start.26 = (bf16[1024,192]{1,0:T(8,128)(2,1)S(1)}, bf16[1024,192]{1,0:T(8,128)(2,1)}, u32[]{:S(2)}, u32[]{:S(2)}) collective-permute-start(bf16[1024,192]{1,0:T(8,128)(2,1)S(1)} %get-tuple-element.238), channel_id=1, source_target_pairs={{0,2},{1,3},{2,0},{3,1},{4,6},{5,7},{6,4},{7,5},{8,10},{9,11},{10,... | collective-permute-start | bytes 1179656 | tf_op jit(solution)/shard_map/ppermute | solution.py:406
  139.6 56.6 %collective-permute-start.25 = (bf16[1024,192]{1,0:T(8,128)(2,1)S(1)}, bf16[1024,192]{1,0:T(8,128)(2,1)}, u32[]{:S(2)}, u32[]{:S(2)}) collective-permute-start(bf16[1024,192]{1,0:T(8,128)(2,1)S(1)} %get-tuple-element.239), channel_id=1, source_target_pairs={{0,1},{1,0},{2,3},{3,2},{4,5},{5,4},{6,7},{7,6},{8,9},{9,8},{10,11... | collective-permute-start | bytes 1179656 | tf_op jit(solution)/shard_map/ppermute | solution.py:402
  169.8 26.3 %collective-permute-start.27 = (bf16[1024,192]{1,0:T(8,128)(2,1)}, bf16[1024,192]{1,0:T(8,128)(2,1)}, u32[]{:S(2)}, u32[]{:S(2)}) collective-permute-start(bf16[1024,192]{1,0:T(8,128)(2,1)} %collective-permute-done.26), channel_id=1, source_target_pairs={{0,1},{1,0},{2,3},{3,2},{4,5},{5,4},{6,7},{7,6},{8,9},{9,8},{10,11... | collective-permute-start | bytes 1179656 | tf_op jit(solution)/shard_map/ppermute | solution.py:402
  170.7 28.9 %collective-permute-start.20 = (bf16[384,768]{1,0:T(8,128)(2,1)}, bf16[384,768]{1,0:T(8,128)(2,1)}, u32[]{:S(2)}, u32[]{:S(2)}) collective-permute-start(bf16[384,768]{1,0:T(8,128)(2,1)} %collective-permute-done.19), channel_id=1, source_target_pairs={{0,4},{4,0},{8,12},{12,8},{16,20},{20,16},{24,28},{28,24},{1,5},{5... | collective-permute-start | bytes 1769480 | tf_op jit(solution)/shard_map/ppermute | solution.py:410
  172.4 28.5 %collective-permute-start.22 = (bf16[384,768]{1,0:T(8,128)(2,1)}, bf16[384,768]{1,0:T(8,128)(2,1)}, u32[]{:S(2)}, u32[]{:S(2)}) collective-permute-start(bf16[384,768]{1,0:T(8,128)(2,1)} %collective-permute-done.21), channel_id=1, source_target_pairs={{0,4},{4,0},{8,12},{12,8},{16,20},{20,16},{24,28},{28,24},{1,5},{5... | collective-permute-start | bytes 1769480 | tf_op jit(solution)/shard_map/ppermute | solution.py:410
  234.7 28.7 %collective-permute-start.53 = (bf16[2,2,2,96,768]{4,3,2,1,0:T(8,128)(2,1)}, bf16[2,2,2,96,768]{4,3,2,1,0:T(8,128)(2,1)}, u32[]{:S(2)}, u32[]{:S(2)}) collective-permute-start(bf16[2,2,2,96,768]{4,3,2,1,0:T(8,128)(2,1)} %bitcast.63), channel_id=1, source_target_pairs={{0,2},{1,3},{2,0},{3,1},{4,6},{5,7},{6,4},{7,5},{8,10},{9,11},{10,... | collective-permute-start | bytes 3538952 | tf_op jit(solution)/shard_map/ppermute | solution.py:406
  242.4 29.2 %collective-permute-start.61 = (bf16[2,2,2,96,768]{4,3,2,1,0:T(8,128)(2,1)}, bf16[2,2,2,96,768]{4,3,2,1,0:T(8,128)(2,1)}, u32[]{:S(2)}, u32[]{:S(2)}) collective-permute-start(bf16[2,2,2,96,768]{4,3,2,1,0:T(8,128)(2,1)} %copy.303), channel_id=1, source_target_pairs={{0,4},{4,0},{8,12},{12,8},{16,20},{20,16},{24,28},{28,24},{1,5},{5... | collective-permute-start | bytes 3538952 | tf_op jit(solution)/shard_map/ppermute | solution.py:410
  243.9 33.0 %collective-permute-start.23 = (bf16[1024,768]{1,0:T(8,128)(2,1)}, bf16[1024,768]{1,0:T(8,128)(2,1)}, u32[]{:S(2)}, u32[]{:S(2)}) collective-permute-start(bf16[1024,768]{1,0:T(8,128)(2,1)} %get-tuple-element.65), channel_id=1, source_target_pairs={{0,1},{1,0},{2,3},{3,2},{4,5},{5,4},{6,7},{7,6},{8,9},{9,8},{10,11... | collective-permute-start | bytes 4718600 | tf_op jit(solution)/shard_map/ppermute | solution.py:402
  245.5 37.6 %collective-permute-start.28 = (bf16[1024,768]{1,0:T(8,128)(2,1)}, bf16[1024,768]{1,0:T(8,128)(2,1)}, u32[]{:S(2)}, u32[]{:S(2)}) collective-permute-start(bf16[1024,768]{1,0:T(8,128)(2,1)} %get-tuple-element.67.refs_1_), channel_id=1, source_target_pairs={{0,1},{1,0},{2,3},{3,2},{4,5},{5,4},{6,7},{7,6},{8,9},{9,8},{10,11... | collective-permute-start | bytes 4718600 | tf_op jit(solution)/shard_map/ppermute | solution.py:402
  265.8 70.1 %collective-permute-start.54 = (bf16[2,2,96,768]{3,2,1,0:T(8,128)(2,1)}, bf16[2,2,96,768]{3,2,1,0:T(8,128)(2,1)}, u32[]{:S(2)}, u32[]{:S(2)}) collective-permute-start(bf16[2,2,96,768]{3,2,1,0:T(8,128)(2,1)} %copy.295), channel_id=1, source_target_pairs={{0,4},{4,0},{8,12},{12,8},{16,20},{20,16},{24,28},{28,24},{1,5},{5... | collective-permute-start | bytes 1769480 | tf_op jit(solution)/shard_map/ppermute | solution.py:410
  275.3 64.2 %collective-permute-start.62 = (bf16[2,2,96,768]{3,2,1,0:T(8,128)(2,1)}, bf16[2,2,96,768]{3,2,1,0:T(8,128)(2,1)}, u32[]{:S(2)}, u32[]{:S(2)}) collective-permute-start(bf16[2,2,96,768]{3,2,1,0:T(8,128)(2,1)} %select_bitcast_fusion.4), channel_id=1, source_target_pairs={{0,8},{4,12},{8,0},{12,4},{16,24},{20,28},{24,16},{28,20},{1,9},{5... | collective-permute-start | bytes 1769480 | tf_op jit(solution)/shard_map/ppermute | solution.py:410
  281.5 60.5 %collective-permute-start.24 = (bf16[1024,192]{1,0:T(8,128)(2,1)}, bf16[1024,192]{1,0:T(8,128)(2,1)}, u32[]{:S(2)}, u32[]{:S(2)}) collective-permute-start(bf16[1024,192]{1,0:T(8,128)(2,1)} %slice_select_fusion.4), channel_id=1, source_target_pairs={{0,2},{1,3},{2,0},{3,1},{4,6},{5,7},{6,4},{7,5},{8,10},{9,11},{10,... | collective-permute-start | bytes 1179656 | tf_op jit(solution)/shard_map/ppermute | solution.py:406
  335.5 48.8 %collective-permute-start.45 = (bf16[2,2,2,96,768]{4,3,2,1,0:T(8,128)(2,1)}, bf16[2,2,2,96,768]{4,3,2,1,0:T(8,128)(2,1)}, u32[]{:S(2)}, u32[]{:S(2)}) collective-permute-start(bf16[2,2,2,96,768]{4,3,2,1,0:T(8,128)(2,1)} %copy.282), channel_id=1, source_target_pairs={{0,8},{4,12},{8,0},{12,4},{16,24},{20,28},{24,16},{28,20},{1,9},{5... | collective-permute-start | bytes 3538952 | tf_op jit(solution)/shard_map/ppermute | solution.py:410
  335.9 50.6 %collective-permute-start.29 = (bf16[1024,768]{1,0:T(8,128)(2,1)}, bf16[1024,768]{1,0:T(8,128)(2,1)}, u32[]{:S(2)}, u32[]{:S(2)}) collective-permute-start(bf16[1024,768]{1,0:T(8,128)(2,1)} %convolution_convert_fusion.7.own), channel_id=1, source_target_pairs={{0,1},{1,0},{2,3},{3,2},{4,5},{5,4},{6,7},{7,6},{8,9},{9,8},{10,11... | collective-permute-start | bytes 4718600 | tf_op jit(solution)/shard_map/ppermute | solution.py:402
  338.0 30.6 %collective-permute-start.55 = (bf16[2,96,768]{2,1,0:T(8,128)(2,1)}, bf16[2,96,768]{2,1,0:T(8,128)(2,1)}, u32[]{:S(2)}, u32[]{:S(2)}) collective-permute-start(bf16[2,96,768]{2,1,0:T(8,128)(2,1)} %select_bitcast_fusion.12), channel_id=1, source_target_pairs={{0,8},{4,12},{8,0},{12,4},{16,24},{20,28},{24,16},{28,20},{1,9},{5... | collective-permute-start | bytes 884744 | tf_op jit(solution)/shard_map/ppermute | solution.py:410
  341.6 30.7 %collective-permute-start.63 = (bf16[2,96,768]{2,1,0:T(8,128)(2,1)}, bf16[2,96,768]{2,1,0:T(8,128)(2,1)}, u32[]{:S(2)}, u32[]{:S(2)}) collective-permute-start(bf16[2,96,768]{2,1,0:T(8,128)(2,1)} %slice_bitcast_fusion.10), channel_id=1, source_target_pairs={{0,2},{1,3},{2,0},{3,1},{4,6},{5,7},{6,4},{7,5},{8,10},{9,11},{10,... | collective-permute-start | bytes 884744 | tf_op jit(solution)/shard_map/ppermute | solution.py:406
  369.6 12.3 %collective-permute-start.56 = (bf16[96,768]{1,0:T(8,128)(2,1)S(1)}, bf16[96,768]{1,0:T(8,128)(2,1)S(1)}, u32[]{:S(2)}, u32[]{:S(2)}) collective-permute-start(bf16[96,768]{1,0:T(8,128)(2,1)S(1)} %select_bitcast_fusion.17), channel_id=1, source_target_pairs={{0,16},{4,20},{8,24},{12,28},{16,0},{20,4},{24,8},{28,12},{1,17},{... | collective-permute-start | bytes 442376 | tf_op jit(solution)/shard_map/ppermute | solution.py:410
  373.4 10.2 %collective-permute-start.64 = (bf16[96,768]{1,0:T(8,128)(2,1)S(1)}, bf16[96,768]{1,0:T(8,128)(2,1)S(1)}, u32[]{:S(2)}, u32[]{:S(2)}) collective-permute-start(bf16[96,768]{1,0:T(8,128)(2,1)S(1)} %select_bitcast_fusion.15), channel_id=1, source_target_pairs={{0,16},{4,20},{8,24},{12,28},{16,0},{20,4},{24,8},{28,12},{1,17},{... | collective-permute-start | bytes 442376 | tf_op jit(solution)/shard_map/ppermute | solution.py:410
  386.1 31.5 %collective-permute-start.46 = (bf16[2,2,96,768]{3,2,1,0:T(8,128)(2,1)S(1)}, bf16[2,2,96,768]{3,2,1,0:T(8,128)(2,1)S(1)}, u32[]{:S(2)}, u32[]{:S(2)}) collective-permute-start(bf16[2,2,96,768]{3,2,1,0:T(8,128)(2,1)S(1)} %copy.284), channel_id=1, source_target_pairs={{0,2},{1,3},{2,0},{3,1},{4,6},{5,7},{6,4},{7,5},{8,10},{9,11},{10,... | collective-permute-start | bytes 1769480 | tf_op jit(solution)/shard_map/ppermute | solution.py:406
  412.1 26.2 %collective-permute-start.49 = (bf16[2,2,2,96,768]{4,3,2,1,0:T(8,128)(2,1)S(1)}, bf16[2,2,2,96,768]{4,3,2,1,0:T(8,128)(2,1)S(1)}, u32[]{:S(2)}, u32[]{:S(2)}) collective-permute-start(bf16[2,2,2,96,768]{4,3,2,1,0:T(8,128)(2,1)S(1)} %bitcast.314), channel_id=1, source_target_pairs={{0,2},{1,3},{2,0},{3,1},{4,6},{5,7},{6,4},{7,5},{8,10},{9,11},{10,... | collective-permute-start | bytes 3538952 | tf_op jit(solution)/shard_map/ppermute | solution.py:406
  413.8 41.6 %collective-permute-start.30 = (bf16[1024,768]{1,0:T(8,128)(2,1)S(1)}, bf16[1024,768]{1,0:T(8,128)(2,1)S(1)}, u32[]{:S(2)}, u32[]{:S(2)}) collective-permute-start(bf16[1024,768]{1,0:T(8,128)(2,1)S(1)} %copy-done.30), channel_id=1, source_target_pairs={{0,1},{1,0},{2,3},{3,2},{4,5},{5,4},{6,7},{7,6},{8,9},{9,8},{10,11... | collective-permute-start | bytes 4718600 | tf_op jit(solution)/shard_map/ppermute | solution.py:402
  419.8 33.3 %collective-permute-start.57 = (bf16[2,2,2,96,768]{4,3,2,1,0:T(8,128)(2,1)S(1)}, bf16[2,2,2,96,768]{4,3,2,1,0:T(8,128)(2,1)S(1)}, u32[]{:S(2)}, u32[]{:S(2)}) collective-permute-start(bf16[2,2,2,96,768]{4,3,2,1,0:T(8,128)(2,1)S(1)} %copy.299), channel_id=1, source_target_pairs={{0,4},{4,0},{8,12},{12,8},{16,20},{20,16},{24,28},{28,24},{1,5},{5... | collective-permute-start | bytes 3538952 | tf_op jit(solution)/shard_map/ppermute | solution.py:410
  439.5 83.6 %collective-permute-start.50 = (bf16[2,2,96,768]{3,2,1,0:T(8,128)(2,1)}, bf16[2,2,96,768]{3,2,1,0:T(8,128)(2,1)}, u32[]{:S(2)}, u32[]{:S(2)}) collective-permute-start(bf16[2,2,96,768]{3,2,1,0:T(8,128)(2,1)} %select_bitcast_fusion.7), channel_id=1, source_target_pairs={{0,4},{4,0},{8,12},{12,8},{16,20},{20,16},{24,28},{28,24},{1,5},{5... | collective-permute-start | bytes 1769480 | tf_op jit(solution)/shard_map/ppermute | solution.py:410
  455.5 69.3 %collective-permute-start.58 = (bf16[2,2,96,768]{3,2,1,0:T(8,128)(2,1)}, bf16[2,2,96,768]{3,2,1,0:T(8,128)(2,1)}, u32[]{:S(2)}, u32[]{:S(2)}) collective-permute-start(bf16[2,2,96,768]{3,2,1,0:T(8,128)(2,1)} %select_bitcast_fusion.5), channel_id=1, source_target_pairs={{0,8},{4,12},{8,0},{12,4},{16,24},{20,28},{24,16},{28,20},{1,9},{5... | collective-permute-start | bytes 1769480 | tf_op jit(solution)/shard_map/ppermute | solution.py:410
  521.0 47.3 %collective-permute-start.41 = (bf16[2,2,2,96,768]{4,3,2,1,0:T(8,128)(2,1)S(1)}, bf16[2,2,2,96,768]{4,3,2,1,0:T(8,128)(2,1)S(1)}, u32[]{:S(2)}, u32[]{:S(2)}) collective-permute-start(bf16[2,2,2,96,768]{4,3,2,1,0:T(8,128)(2,1)S(1)} %copy.269), channel_id=1, source_target_pairs={{0,8},{4,12},{8,0},{12,4},{16,24},{20,28},{24,16},{28,20},{1,9},{5... | collective-permute-start | bytes 3538952 | tf_op jit(solution)/shard_map/ppermute | solution.py:410
  523.1 47.6 %collective-permute-start.31 = (bf16[1024,768]{1,0:T(8,128)(2,1)S(1)}, bf16[1024,768]{1,0:T(8,128)(2,1)S(1)}, u32[]{:S(2)}, u32[]{:S(2)}) collective-permute-start(bf16[1024,768]{1,0:T(8,128)(2,1)S(1)} %copy-done.31), channel_id=1, source_target_pairs={{0,1},{1,0},{2,3},{3,2},{4,5},{5,4},{6,7},{7,6},{8,9},{9,8},{10,11... | collective-permute-start | bytes 4718600 | tf_op jit(solution)/shard_map/ppermute | solution.py:402
  524.4 29.1 %collective-permute-start.51 = (bf16[2,96,768]{2,1,0:T(8,128)(2,1)S(1)}, bf16[2,96,768]{2,1,0:T(8,128)(2,1)S(1)}, u32[]{:S(2)}, u32[]{:S(2)}) collective-permute-start(bf16[2,96,768]{2,1,0:T(8,128)(2,1)S(1)} %fusion.29), channel_id=1, source_target_pairs={{0,8},{4,12},{8,0},{12,4},{16,24},{20,28},{24,16},{28,20},{1,9},{5... | collective-permute-start | bytes 884744 | tf_op jit(solution)/shard_map/ppermute | solution.py:410
  526.0 30.3 %collective-permute-start.59 = (bf16[2,96,768]{2,1,0:T(8,128)(2,1)S(1)}, bf16[2,96,768]{2,1,0:T(8,128)(2,1)S(1)}, u32[]{:S(2)}, u32[]{:S(2)}) collective-permute-start(bf16[2,96,768]{2,1,0:T(8,128)(2,1)S(1)} %slice_bitcast_fusion.12), channel_id=1, source_target_pairs={{0,2},{1,3},{2,0},{3,1},{4,6},{5,7},{6,4},{7,5},{8,10},{9,11},{10,... | collective-permute-start | bytes 884744 | tf_op jit(solution)/shard_map/ppermute | solution.py:406
  553.7 11.5 %collective-permute-start.52 = (bf16[96,768]{1,0:T(8,128)(2,1)S(1)}, bf16[96,768]{1,0:T(8,128)(2,1)S(1)}, u32[]{:S(2)}, u32[]{:S(2)}) collective-permute-start(bf16[96,768]{1,0:T(8,128)(2,1)S(1)} %select_bitcast_fusion.18), channel_id=1, source_target_pairs={{0,16},{4,20},{8,24},{12,28},{16,0},{20,4},{24,8},{28,12},{1,17},{... | collective-permute-start | bytes 442376 | tf_op jit(solution)/shard_map/ppermute | solution.py:410
  556.5 10.8 %collective-permute-start.60 = (bf16[96,768]{1,0:T(8,128)(2,1)S(1)}, bf16[96,768]{1,0:T(8,128)(2,1)S(1)}, u32[]{:S(2)}, u32[]{:S(2)}) collective-permute-start(bf16[96,768]{1,0:T(8,128)(2,1)S(1)} %select_bitcast_fusion.16), channel_id=1, source_target_pairs={{0,16},{4,20},{8,24},{12,28},{16,0},{20,4},{24,8},{28,12},{1,17},{... | collective-permute-start | bytes 442376 | tf_op jit(solution)/shard_map/ppermute | solution.py:410
  570.6 36.5 %collective-permute-start.42 = (bf16[2,2,96,768]{3,2,1,0:T(8,128)(2,1)}, bf16[2,2,96,768]{3,2,1,0:T(8,128)(2,1)}, u32[]{:S(2)}, u32[]{:S(2)}) collective-permute-start(bf16[2,2,96,768]{3,2,1,0:T(8,128)(2,1)} %copy.271), channel_id=1, source_target_pairs={{0,2},{1,3},{2,0},{3,1},{4,6},{5,7},{6,4},{7,5},{8,10},{9,11},{10,... | collective-permute-start | bytes 1769480 | tf_op jit(solution)/shard_map/ppermute | solution.py:406
  591.6 29.9 %collective-permute-start.32 = (bf16[1024,192]{1,0:T(8,128)(2,1)S(1)}, bf16[1024,192]{1,0:T(8,128)(2,1)}, u32[]{:S(2)}, u32[]{:S(2)}) collective-permute-start(bf16[1024,192]{1,0:T(8,128)(2,1)S(1)} %fusion.15), channel_id=1, source_target_pairs={{0,2},{1,3},{2,0},{3,1},{4,6},{5,7},{6,4},{7,5},{8,10},{9,11},{10,... | collective-permute-start | bytes 1179656 | tf_op jit(solution)/shard_map/ppermute | solution.py:406
  (93 other events, 686.3 us)
